TPU v7x, 32 devices: a whole 2x2x4 slice. The times are simulated.
32 devices in a mesh: rows: 4 (over y, x), seq: 8 (over z, core).
Axes of the slice: x: 2, y: 2, z: 4, core: 2. Of those that a mesh axis runs over, the one named last changes fastest.
Arguments:
- residual_in: float32 [32, 1024, 512], P('rows', 'seq'), may hold values from -6 to 6
- cotangent: float32 [32, 1024, 512], P('rows', 'seq'), may hold values from -6 to 6
- segments: int32 [32, 1024], P('rows'), may hold values from 0 to 7, never falling along the last dimension, each value on 1 to 512 neighbouring positions
- owners: int32 [96], replicated, may hold values from 0 to 7, as said below
- master_tiles: float32 [128, 512, 128], P('seq'), may hold values from -0.53033009 to 0.53033009, as said below
- first_tiles: float32 [128, 512, 128], P('seq'), may hold values from -0.0024414062 to 0.0024414062
- second_tiles: float32 [128, 512, 128], P('seq'), may hold values from 1.5873903e-07 to 6.349561e-07
- norm_params: float32 [8, 512], replicated, may hold values from -2 to 2
- norm_first: float32 [8, 512], replicated, may hold values from -0.009765625 to 0.009765625
- norm_second: float32 [8, 512], replicated, may hold values from 2.5398244e-06 to 1.0159298e-05
Outputs:
- residual_out: float32 [32, 1024, 512], P('rows', 'seq')
- input_grad: float32 [32, 1024, 512], P('rows', 'seq')
- tile_grads: float32 [128, 512, 128], P('seq')
- grad_norm: float32 [1], replicated
- new_first: float32 [128, 512, 128], P('seq')
- new_second: float32 [128, 512, 128], P('seq')
- new_master: float32 [128, 512, 128], P('seq')
- new_copies: bfloat16 [128, 512, 128], P('seq')
- norm_grads: float32 [8, 512], replicated
- new_norm_first: float32 [8, 512], replicated
- new_norm_second: float32 [8, 512], replicated
- new_norm_params: float32 [8, 512], replicated
Inputs may be any that keep to these rules, and one draw needn't show every extreme that they name: `owners`: no device owns more than 16 tiles, and one device owns exactly 16. `segments`: along a row the document numbers never fall; a document has 1 to 512 positions and some document exactly 512. `master_tiles`: slot 16 d + n holds the tile with the n-th smallest number among those owned by device d; slots that hold no tile are ignored.
All inputs are finite; a program needn't handle non-finite values.
Results may differ from a plain program's by a relative error of at most 0.013.
Values may be sent and summed in bfloat16 or wider, within the bound.
A program may use at most 256 MiB of HBM per device.

v0:
```python
import jax
import jax.numpy as jnp
from jax import lax
from jax.sharding import PartitionSpec as P

HEADS = 8
LAYERS = 2
STEP = 5


def norm_layer(values, gain, offset):
    center = values - jnp.mean(values, axis=-1, keepdims=True)
    spread = jnp.mean(center * center, axis=-1, keepdims=True)
    return center * lax.rsqrt(spread + 1e-05) * gain + offset


def matmul(left, right):
    return jnp.dot(left, right, preferred_element_type=jnp.float32)


def left_product(left, right):
    return lax.dot_general(
        left, right, (((0,), (0,)), ((), ())), preferred_element_type=jnp.float32
    )


def right_product(left, right):
    return lax.dot_general(
        left, right, (((1,), (1,)), ((), ())), preferred_element_type=jnp.float32
    )


def assemble(weight_tiles, layer_number):
    first_tile = 48 * layer_number
    model_width = weight_tiles.shape[1]
    qkv_weight = (
        weight_tiles[first_tile : first_tile + 12].transpose(1, 0, 2).reshape(model_width, -1)
    )
    out_weight = (
        weight_tiles[first_tile + 12 : first_tile + 16].transpose(1, 0, 2).reshape(model_width, -1)
    )
    up_weight = (
        weight_tiles[first_tile + 16 : first_tile + 32].transpose(1, 0, 2).reshape(model_width, -1)
    )
    down_block = weight_tiles[first_tile + 32 : first_tile + 48].reshape(4, 4, model_width, -1)
    down_weight = down_block.transpose(0, 2, 1, 3).reshape(4 * model_width, model_width)
    return (qkv_weight, out_weight, up_weight, down_weight)


def split_tiles(qkv_grad, out_grad, up_grad, down_grad, tile_width):
    model_width = qkv_grad.shape[0]
    pieces = [
        qkv_grad.reshape(model_width, -1, tile_width).transpose(1, 0, 2),
        out_grad.reshape(model_width, -1, tile_width).transpose(1, 0, 2),
        up_grad.reshape(model_width, -1, tile_width).transpose(1, 0, 2),
        down_grad.reshape(4, model_width, 4, tile_width)
        .transpose(0, 2, 1, 3)
        .reshape(16, model_width, tile_width),
    ]
    return jnp.concatenate(pieces, axis=0)


def attend_forward(queries, key_rows, value_rows, doc_ids, block_rows, scale):
    length = queries.shape[0]

    def one_block(number):
        first_row = number * block_rows
        query_block = lax.dynamic_slice_in_dim(queries, first_row, block_rows, 0)
        doc_block = lax.dynamic_slice_in_dim(doc_ids, first_row, block_rows, 0)
        same_doc = doc_block[:, None] == doc_ids[None, :]
        scores = jnp.where(same_doc, right_product(query_block, key_rows) * scale, -1e30)
        largest = jnp.max(scores, axis=-1, keepdims=True)
        row_total = jnp.sum(jnp.exp(scores - largest), axis=-1, keepdims=True)
        logsum = largest + jnp.log(row_total)
        weights = jnp.where(same_doc, jnp.exp(scores - logsum), 0.0).astype(jnp.bfloat16)
        return (matmul(weights, value_rows).astype(jnp.bfloat16), logsum[:, 0])

    outputs, logsums = lax.map(one_block, jnp.arange(length // block_rows))
    return (outputs.reshape(length, -1), logsums.reshape(length))


def attend_backward(queries, key_rows, value_rows, doc_ids, logsums, out_grads, block_rows, scale):
    length, head_dim = queries.shape

    def one_block(carry, number):
        key_grad, value_grad = carry
        first_row = number * block_rows
        query_block = lax.dynamic_slice_in_dim(queries, first_row, block_rows, 0)
        doc_block = lax.dynamic_slice_in_dim(doc_ids, first_row, block_rows, 0)
        logsum_block = lax.dynamic_slice_in_dim(logsums, first_row, block_rows, 0)
        grad_block = lax.dynamic_slice_in_dim(out_grads, first_row, block_rows, 0)
        same_doc = doc_block[:, None] == doc_ids[None, :]
        scores = jnp.where(same_doc, right_product(query_block, key_rows) * scale, -1e30)
        probs = jnp.where(same_doc, jnp.exp(scores - logsum_block[:, None]), 0.0)
        prob_grad = right_product(grad_block, value_rows)
        inner_sum = jnp.sum(probs * prob_grad, axis=-1, keepdims=True)
        score_grad = (probs * (prob_grad - inner_sum)).astype(jnp.bfloat16)
        query_grad = matmul(score_grad, key_rows) * scale
        key_grad = key_grad + left_product(score_grad, query_block) * scale
        value_grad = value_grad + left_product(probs.astype(jnp.bfloat16), grad_block)
        return ((key_grad, value_grad), query_grad)

    zeros_block = jnp.zeros((length, head_dim), jnp.float32)
    (key_grad, value_grad), query_grads = lax.scan(
        one_block, (zeros_block, zeros_block), jnp.arange(length // block_rows)
    )
    stacked = jnp.stack([query_grads.reshape(length, head_dim), key_grad, value_grad], axis=1)
    return stacked.astype(jnp.bfloat16)


def adamw(weight, grad, first, second, learn_rate, correction):
    first = 0.5 * first + 0.5 * grad
    second = 0.5 * second + 0.5 * grad * grad
    update = first / correction / (jnp.sqrt(second / correction) + 1e-08)
    return (weight - learn_rate * (update + 0.01 * weight), first, second)


def local(
    residual_in,
    cotangent,
    segments,
    owners,
    master_tiles,
    first_tiles,
    second_tiles,
    norm_params,
    norm_first,
    norm_second,
):
    local_rows, positions, model_width = residual_in.shape
    seq_devices = lax.axis_size("seq")
    seq_index = lax.axis_index("seq")
    head_dim = model_width // HEADS
    group_count = seq_devices // HEADS
    group_rows = local_rows // group_count
    length = positions * seq_devices
    block_rows = min(512, length)
    scale = head_dim ** (-0.5)
    tile_total = owners.shape[0]
    capacity = master_tiles.shape[0]
    tile_width = master_tiles.shape[2]
    places = jnp.arange(tile_total, dtype=jnp.int32)
    before = (owners[None, :] == owners[:, None]) & (places[None, :] < places[:, None])
    ranks = jnp.sum(before.astype(jnp.int32), axis=1)
    slot_ids = owners * capacity + ranks
    local_slots = jnp.arange(capacity, dtype=jnp.int32)
    matches = (owners[:, None] == seq_index) & (ranks[:, None] == local_slots[None, :])
    chosen = jnp.sum(jnp.where(matches, places[:, None], 0), axis=0)
    present = jnp.any(matches, axis=0)
    copies = lax.all_gather(master_tiles.astype(jnp.bfloat16), "seq", axis=0, tiled=True)
    weight_tiles = jnp.take(copies, slot_ids, axis=0)
    my_group = seq_index // HEADS
    doc_rows = lax.dynamic_slice_in_dim(segments, my_group * group_rows, group_rows, 0)
    hidden = residual_in.reshape(-1, model_width)
    saved = []
    for layer_number in range(LAYERS):
        qkv_weight, out_weight, up_weight, down_weight = assemble(weight_tiles, layer_number)
        params = norm_params[4 * layer_number : 4 * layer_number + 4]
        normed, first_pull = jax.vjp(norm_layer, hidden, params[0], params[1])
        normed_low = normed.astype(jnp.bfloat16)
        packed = matmul(normed_low, qkv_weight).astype(jnp.bfloat16)
        outgoing = packed.reshape(group_count, group_rows, positions, 3, HEADS, head_dim)
        outgoing = outgoing.transpose(0, 4, 1, 2, 3, 5).reshape(
            seq_devices, group_rows, positions * 3 * head_dim
        )
        arrived = lax.all_to_all(outgoing, "seq", split_axis=0, concat_axis=2, tiled=True).reshape(
            group_rows, length, 3, head_dim
        )

        def forward_item(items):
            return attend_forward(
                items[0][:, 0], items[0][:, 1], items[0][:, 2], items[1], block_rows, scale
            )

        attended, logsums = lax.map(forward_item, (arrived, doc_rows))
        returning = attended.reshape(1, group_rows, seq_devices, positions * head_dim)
        mixed = lax.all_to_all(returning, "seq", split_axis=2, concat_axis=0, tiled=True)
        mixed = (
            mixed.reshape(group_count, HEADS, group_rows, positions, head_dim)
            .transpose(0, 2, 3, 1, 4)
            .reshape(-1, model_width)
        )
        middle = hidden + matmul(mixed, out_weight)
        normed_two, second_pull = jax.vjp(norm_layer, middle, params[2], params[3])
        normed_two_low = normed_two.astype(jnp.bfloat16)
        inner = matmul(normed_two_low, up_weight)
        active = jax.nn.gelu(inner).astype(jnp.bfloat16)
        hidden = middle + matmul(active, down_weight)
        saved.append(
            (
                first_pull,
                normed_low,
                arrived,
                logsums,
                mixed,
                second_pull,
                normed_two_low,
                inner,
                active,
            )
        )
    grad = cotangent.reshape(-1, model_width)
    tile_parts = [None] * LAYERS
    norm_parts = [None] * LAYERS
    for layer_number in reversed(range(LAYERS)):
        (
            first_pull,
            normed_low,
            arrived,
            logsums,
            mixed,
            second_pull,
            normed_two_low,
            inner,
            active,
        ) = saved[layer_number]
        qkv_weight, out_weight, up_weight, down_weight = assemble(weight_tiles, layer_number)
        grad_low = grad.astype(jnp.bfloat16)
        down_grad = left_product(active, grad_low)
        active_grad = right_product(grad_low, down_weight)
        inner_grad = jax.vjp(jax.nn.gelu, inner)[1](active_grad)[0].astype(jnp.bfloat16)
        up_grad = left_product(normed_two_low, inner_grad)
        middle_part, gain_two, offset_two = second_pull(right_product(inner_grad, up_weight))
        middle_grad = grad + middle_part
        middle_low = middle_grad.astype(jnp.bfloat16)
        out_grad = left_product(mixed, middle_low)
        mixed_grad = right_product(middle_low, out_weight).astype(jnp.bfloat16)
        sending = mixed_grad.reshape(group_count, group_rows, positions, HEADS, head_dim)
        sending = sending.transpose(0, 3, 1, 2, 4).reshape(
            seq_devices, group_rows, positions * head_dim
        )
        head_grads = lax.all_to_all(
            sending, "seq", split_axis=0, concat_axis=2, tiled=True
        ).reshape(group_rows, length, head_dim)

        def backward_item(items):
            arrived_row, doc_row, logsum_row, grad_row = items
            return attend_backward(
                arrived_row[:, 0],
                arrived_row[:, 1],
                arrived_row[:, 2],
                doc_row,
                logsum_row,
                grad_row,
                block_rows,
                scale,
            )

        packed_grads = lax.map(backward_item, (arrived, doc_rows, logsums, head_grads))
        coming = lax.all_to_all(
            packed_grads.reshape(1, group_rows, seq_devices, positions * 3 * head_dim),
            "seq",
            split_axis=2,
            concat_axis=0,
            tiled=True,
        )
        qkv_grad = coming.reshape(group_count, HEADS, group_rows, positions, 3, head_dim)
        qkv_grad = qkv_grad.transpose(0, 2, 3, 4, 1, 5).reshape(-1, 3 * model_width)
        qkv_weight_grad = left_product(normed_low, qkv_grad)
        input_part, gain_one, offset_one = first_pull(right_product(qkv_grad, qkv_weight))
        grad = middle_grad + input_part
        tile_parts[layer_number] = split_tiles(
            qkv_weight_grad, out_grad, up_grad, down_grad, tile_width
        )
        norm_parts[layer_number] = jnp.stack([gain_one, offset_one, gain_two, offset_two])
    dense = jnp.concatenate(tile_parts, axis=0)
    norm_part = jnp.concatenate(norm_parts, axis=0)
    piece = lax.psum_scatter(
        dense.reshape(-1, tile_width), ("rows", "seq"), scatter_dimension=0, tiled=True
    )
    squares, norm_sum = lax.psum((jnp.sum(piece * piece), norm_part), ("rows", "seq"))
    summed = (
        lax.all_gather(piece.astype(jnp.bfloat16), ("rows", "seq"), axis=0, tiled=True)
        .astype(piece.dtype)
        .reshape(dense.shape)
    )
    owned = jnp.take(summed, chosen, axis=0)
    keep = present[:, None, None]
    owned = jnp.where(keep, owned, 0.0)
    total = jnp.sqrt(squares + jnp.sum(norm_sum * norm_sum))
    factor = 1.0 / jnp.maximum(total, 1.0)
    clipped = owned * factor
    norm_clip = norm_sum * factor
    correction = 1.0 - 0.5**STEP
    new_weight, new_first_rows, new_second_rows = adamw(
        master_tiles, clipped, first_tiles, second_tiles, 0.05, correction
    )
    new_weight = jnp.where(keep, new_weight, 0.0)
    new_first_rows = jnp.where(keep, new_first_rows, 0.0)
    new_second_rows = jnp.where(keep, new_second_rows, 0.0)
    new_norm, new_norm_f, new_norm_s = adamw(
        norm_params, norm_clip, norm_first, norm_second, 0.25, correction
    )
    return (
        hidden.reshape(local_rows, positions, model_width),
        grad.reshape(local_rows, positions, model_width),
        clipped,
        total[None],
        new_first_rows,
        new_second_rows,
        new_weight,
        new_weight.astype(jnp.bfloat16),
        norm_clip,
        new_norm_f,
        new_norm_s,
        new_norm,
    )


def solution(mesh):
    placed = (
        P("rows", "seq", None),
        P("rows", "seq", None),
        P("rows", None),
        P(),
        P("seq", None, None),
        P("seq", None, None),
        P("seq", None, None),
        P(),
        P(),
        P(),
    )
    return jax.shard_map(
        local,
        mesh=mesh,
        in_specs=placed,
        out_specs=(
            P("rows", "seq", None),
            P("rows", "seq", None),
            P("seq", None, None),
            P(),
            P("seq", None, None),
            P("seq", None, None),
            P("seq", None, None),
            P("seq", None, None),
            P(),
            P(),
            P(),
            P(),
        ),
        check_vma=False,
    )
```

profile of v0, /device:TPU:0, one launch (start us, length us, event | category | flops | bytes accessed | tf_op | source)
XLA Modules:
  0.0 1697.1 jit_solution(15735014790983426228)
XLA Ops:
  17.2 147.9 %all-gather.3.cloned.1.call-done = bf16[128,512,128]{2,1,0:T(8,128)(2,1)} async-done(((bf16[16,512,128]{2,1,0:T(8,128)(2,1)}), bf16[128,512,128]{2,1,0:T(8,128)(2,1)}) %all-gather.3.cloned.1.call-update) | async-done | bytes 16777232 | tf_op jit(solution)/shard_map/all_gather | solution.py:150
  165.1 12.7 gather_fusion
  212.6 10.4 reshape.599
  227.1 71.4 %all-to-all-done = bf16[8,8,24576]{2,1,0:T(8,128)(2,1)S(1)} async-done(((bf16[8,8,24576]{2,1,0:T(8,128)(2,1)}), bf16[8,8,24576]{2,1,0:T(8,128)(2,1)S(1)}, u32[]{:S(2)}, u32[]{:S(2)}) %all-to-all-start) | async-done | bytes 3145760 | tf_op jit(solution)/shard_map/all_to_all | solution.py:166
  301.9 10.4 reshape.600
  320.8 63.0 %while.99 = (s32[]{:T(128)}, bf16[8,1024,64]{2,1,0:T(8,128)(2,1)S(1)}, f32[8,1024]{1,0:T(8,128)S(1)}, bf16[8,1024,3,64]{3,1,2,0:T(8,128)(2,1)}, s32[8,1024]{1,0:...) while((s32[]{:T(128)}, ...), condition=%wide.region_8.9_spmd, body=%wide.region_3.8_spmd.sunk | while | flops 139492864 | bytes 9431484 | solution.py:175
  474.0 71.5 %all-to-all-done.2 = bf16[8,8,24576]{2,1,0:T(8,128)(2,1)} async-done(((bf16[8,8,24576]{2,1,0:T(8,128)(2,1)}), bf16[8,8,24576]{2,1,0:T(8,128)(2,1)}, u32[]{:S(2)}, u32[]{:S(2)}) %all-to-all-start.2) | async-done | bytes 3145760 | tf_op jit(solution)/shard_map/all_to_all | solution.py:166
  550.8 10.5 reshape.611
  570.5 69.8 %while.101 = (s32[]{:T(128)}, bf16[8,1024,64]{2,1,0:T(8,128)(2,1)}, f32[8,1024]{1,0:T(8,128)S(1)}, bf16[8,1024,3,64]{3,1,2,0:T(8,128)(2,1)}, s32[8,1024]{1,0:T(8...) while((s32[]{:T(128)}, bf16[8,1024,64]{2,1,0:T(8,128)(2,1)}, ...), condition=%wide.region_18.19_spmd, body=%wide.region_13.18_spmd.sunk | while | flops 139492864 | bytes 9300412 | solution.py:175
  665.3 10.4 all-to-all-done.3
  715.6 26.5 %all-to-all-done.4 = bf16[8,8,8192]{2,1,0:T(8,128)(2,1)S(1)} async-done(((bf16[8,8,8192]{2,1,0:T(8,128)(2,1)}), bf16[8,8,8192]{2,1,0:T(8,128)(2,1)S(1)}, u32[]{:S(2)}, u32[]{:S(2)}) %all-to-all-start.4) | async-done | bytes 1048608 | tf_op jit(solution)/shard_map/all_to_all | solution.py:232
  748.9 104.1 %while.103 = (s32[]{:T(128)}, bf16[8,1024,3,64]{1,3,2,0:T(8,128)(2,1)}, bf16[8,1024,3,64]{3,1,2,0:T(8,128)(2,1)}, s32[8,1024]{1,0:T(8,128)S(1)}, f32[8,1024]{1,0...) while((s32[]{:T(128)}, ...), condition=%wide.region_27.28_spmd, body=%wide.region_23.27_spmd.sunk | while | flops 342982144 | bytes 30577220 | solution.py:249
  853.1 12.5 copy.235
  876.6 74.2 %all_to_all.120 = bf16[1,8,8,24576]{3,1,0,2:T(8,128)(2,1)S(1)} all-to-all(bf16[1,8,8,24576]{3,1,0,2:T(8,128)(2,1)S(1)} %copy.236), channel_id=1, replica_groups=mesh['rows'=4,'seq'=8] {'seq'}, dimensions={2} | all-to-all | bytes 6291456 | tf_op jit(solution)/shard_map/all_to_all | solution.py:250
  1016.5 26.5 %all-to-all-done.6 = bf16[8,8,8192]{2,1,0:T(8,128)(2,1)S(1)} async-done(((bf16[8,8,8192]{2,1,0:T(8,128)(2,1)}), bf16[8,8,8192]{2,1,0:T(8,128)(2,1)S(1)}, u32[]{:S(2)}, u32[]{:S(2)}) %all-to-all-start.6) | async-done | bytes 1048608 | tf_op jit(solution)/shard_map/all_to_all | solution.py:232
  1049.9 102.7 %while.105 = (s32[]{:T(128)}, bf16[8,1024,3,64]{1,3,2,0:T(8,128)(2,1)}, bf16[8,1024,3,64]{3,1,2,0:T(8,128)(2,1)}, s32[8,1024]{1,0:T(8,128)S(1)}, f32[8,1024]{1,0...) while((s32[]{:T(128)}, ...), condition=%wide.region_36.37_spmd, body=%wide.region_32.36_spmd.sunk | while | flops 342982144 | bytes 30577220 | solution.py:249
  1152.7 12.5 copy.244
  1228.3 25.8 %all-to-all-done.7 = bf16[1,8,8,24576]{3,1,0,2:T(8,128)(2,1)} async-done(((bf16[1,8,8,24576]{3,1,0,2:T(8,128)(2,1)}), bf16[1,8,8,24576]{3,1,0,2:T(8,128)(2,1)}, u32[]{:S(2)}, u32[]{:S(2)}) %all-to-all-start.7) | async-done | bytes 3145760 | tf_op jit(solution)/shard_map/all_to_all | solution.py:250
  1254.1 10.6 reshape.631
  1302.9 244.4 %reduce-scatter.2.cloned.1.call-done = f32[1536,128]{1,0:T(8,128)} async-done(((f32[49152,128]{1,0:T(8,128)}), f32[1536,128]{1,0:T(8,128)}) %reduce-scatter.2.cloned.1.call-update) | async-done | bytes 786448 | tf_op jit(solution)/shard_map/reduce_scatter | solution.py:268
  1579.8 42.7 %all-reduce = (f32[]{:T(128)}, f32[8,512]{1,0:T(8,128)S(1)}) all-reduce(f32[]{:T(128)} %get-tuple-element.743, f32[8,512]{1,0:T(8,128)S(1)} %concatenate.23), channel_id=1, replica_groups=mesh['rows'=4,'seq'=8] {'rows','seq'}, use_global_device_ids=true, to_apply=%region_43.44 | all-reduce | flops 4097 | bytes 32776 | tf_op jit(solution)/shard_map/psum | solution.py:271
  1625.1 23.5 %all-gather.5.cloned.1.call-done = bf16[49152,128]{1,0:T(8,128)(2,1)} async-done(((bf16[1536,128]{1,0:T(8,128)(2,1)}), bf16[49152,128]{1,0:T(8,128)(2,1)}) %all-gather.5.cloned.1.call-update) | async-done | bytes 12582928 | tf_op jit(solution)/shard_map/all_gather | solution.py:273
  1648.6 14.2 convert.25
  1662.8 11.0 gather_fusion.1
  (1384 shorter events, 1000.4 us)
Async XLA Ops:
  7.2 157.9 %all-gather.3.cloned.1.call-start = ((), (), s32[]{:S(2)}) async-start(), calls=%async_computation.9 | async-start | bytes 18874368 | tf_op jit(solution)/shard_map/all_gather | solution.py:150
  15.3 410.5 %copy-start.97 = (f32[1,512]{1,0:T(1,128)}, f32[1,512]{1,0:T(1,128)S(1)}, u32[]{:S(2)}) copy-start(f32[1,512]{1,0:T(1,128)S(1)} %get-tuple-element.748) | copy-start | bytes 6148
  15.3 410.5 %copy-start.110 = (f32[1,512]{1,0:T(1,128)}, f32[1,512]{1,0:T(1,128)S(1)}, u32[]{:S(2)}) copy-start(f32[1,512]{1,0:T(1,128)S(1)} %get-tuple-element.747) | copy-start | bytes 6148
  15.3 419.1 %copy-start.94 = (f32[1,512]{1,0:T(1,128)}, f32[1,512]{1,0:T(1,128)S(1)}, u32[]{:S(2)}) copy-start(f32[1,512]{1,0:T(1,128)S(1)} %get-tuple-element.746) | copy-start | bytes 6148
  15.3 419.1 %copy-start.108 = (f32[1,512]{1,0:T(1,128)}, f32[1,512]{1,0:T(1,128)S(1)}, u32[]{:S(2)}) copy-start(f32[1,512]{1,0:T(1,128)S(1)} %get-tuple-element.745) | copy-start | bytes 6148
  222.9 75.6 %all-to-all-start = ((bf16[8,8,24576]{2,1,0:T(8,128)(2,1)}), bf16[8,8,24576]{2,1,0:T(8,128)(2,1)S(1)}, u32[]{:S(2)}, u32[]{:S(2)}) async-start(bf16[8,8,24576]{2,1,0:T(8,128)(2,1)} %reshape.599), calls=%async_computation | async-start | bytes 6291456 | tf_op jit(solution)/shard_map/all_to_all | solution.py:166
  387.7 30.1 %all-to-all-start.1 = ((bf16[1,8,8,8192]{3,1,0,2:T(8,128)(2,1)}), bf16[1,8,8,8192]{3,1,0,2:T(8,128)(2,1)S(1)}, u32[]{:S(2)}, u32[]{:S(2)}) async-start(bf16[1,8,8,8192]{3,1,0,2:T(8,128)(2,1)} %copy.213), calls=%async_computation.1 | async-start | bytes 2097152 | tf_op jit(solution)/shard_map/all_to_all | solution.py:177
  393.2 30.0 %copy-start = (f32[1024,512]{0,1:T(8,128)}, f32[1024,512]{0,1:T(8,128)S(1)}, u32[]{:S(2)}) copy-start(f32[1024,512]{0,1:T(8,128)S(1)} %copy.262) | copy-start | bytes 6291460
  434.0 247.0 %copy-start.2 = (f32[1024,512]{0,1:T(8,128)}, f32[1024,512]{0,1:T(8,128)S(1)}, u32[]{:S(2)}) copy-start(f32[1024,512]{0,1:T(8,128)S(1)} %get-tuple-element.760) | copy-start | bytes 6291460
  469.3 76.2 %all-to-all-start.2 = ((bf16[8,8,24576]{2,1,0:T(8,128)(2,1)}), bf16[8,8,24576]{2,1,0:T(8,128)(2,1)}, u32[]{:S(2)}, u32[]{:S(2)}) async-start(bf16[8,8,24576]{2,1,0:T(8,128)(2,1)} %reshape.610), calls=%async_computation.2 | async-start | bytes 6291456 | tf_op jit(solution)/shard_map/all_to_all | solution.py:166
  645.2 30.5 %all-to-all-start.3 = ((bf16[1,8,8,8192]{3,1,0,2:T(8,128)(2,1)}), bf16[1,8,8,8192]{3,1,0,2:T(8,128)(2,1)S(1)}, u32[]{:S(2)}, u32[]{:S(2)}) async-start(bf16[1,8,8,8192]{3,1,0,2:T(8,128)(2,1)} %copy.223), calls=%async_computation.3 | async-start | bytes 2097152 | tf_op jit(solution)/shard_map/all_to_all | solution.py:177
  683.2 20.2 %copy-start.12 = (f32[1024,512]{0,1:T(8,128)}, f32[1024,512]{0,1:T(8,128)S(1)}, u32[]{:S(2)}) copy-start(f32[1024,512]{0,1:T(8,128)S(1)} %get-tuple-element.762) | copy-start | bytes 6291460
  683.2 20.2 %copy-start.85 = (f32[1024]{0:T(1024)}, f32[1024]{0:T(1024)S(1)}, u32[]{:S(2)}) copy-start(f32[1024]{0:T(1024)S(1)} %broadcast_multiply_fusion.1) | copy-start | bytes 12292
  683.5 19.9 %copy-start.102 = (f32[1024]{0:T(1024)}, f32[1024]{0:T(1024)S(1)}, u32[]{:S(2)}) copy-start(f32[1024]{0:T(1024)S(1)} %fusion.118) | copy-start | bytes 12292
  711.8 30.3 %all-to-all-start.4 = ((bf16[8,8,8192]{2,1,0:T(8,128)(2,1)}), bf16[8,8,8192]{2,1,0:T(8,128)(2,1)S(1)}, u32[]{:S(2)}, u32[]{:S(2)}) async-start(bf16[8,8,8192]{2,1,0:T(8,128)(2,1)} %reshape.622), calls=%async_computation.4 | async-start | bytes 2097152 | tf_op jit(solution)/shard_map/all_to_all | solution.py:232
  1013.0 30.1 %all-to-all-start.6 = ((bf16[8,8,8192]{2,1,0:T(8,128)(2,1)}), bf16[8,8,8192]{2,1,0:T(8,128)(2,1)S(1)}, u32[]{:S(2)}, u32[]{:S(2)}) async-start(bf16[8,8,8192]{2,1,0:T(8,128)(2,1)} %reshape.628), calls=%async_computation.6 | async-start | bytes 2097152 | tf_op jit(solution)/shard_map/all_to_all | solution.py:232
  1177.8 76.3 %all-to-all-start.7 = ((bf16[1,8,8,24576]{3,1,0,2:T(8,128)(2,1)}), bf16[1,8,8,24576]{3,1,0,2:T(8,128)(2,1)}, u32[]{:S(2)}, u32[]{:S(2)}) async-start(bf16[1,8,8,24576]{3,1,0,2:T(8,128)(2,1)} %copy.245), calls=%async_computation.7 | async-start | bytes 6291456 | tf_op jit(solution)/shard_map/all_to_all | solution.py:250
  1182.6 364.6 %reduce-scatter.2.cloned.1.call-start = ((), (), s32[]{:S(2)}) async-start(), calls=%async_computation.10 | async-start | bytes 25952256 | tf_op jit(solution)/shard_map/reduce_scatter | solution.py:268
  1302.8 247.3 %copy-start.120 = (s32[96]{0:T(128)S(1)}, s32[96]{0:T(128)}, u32[]{:S(2)}) copy-start(s32[96]{0:T(128)} %copy-done.119) | copy-start | bytes 1156
  1302.8 247.3 %copy-start.121 = (pred[96]{0:T(512)(128)(4,1)S(1)}, pred[96]{0:T(512)(128)(4,1)}, u32[]{:S(2)}) copy-start(pred[96]{0:T(512)(128)(4,1)} %get-tuple-element.756) | copy-start | bytes 292
  1302.8 345.8 %all-gather.5.cloned.1.call-start = ((), (), s32[]{:S(2)}) async-start(), calls=%async_computation.11 | async-start | bytes 12976128 | tf_op jit(solution)/shard_map/all_gather | solution.py:273
  1576.8 47.7 %copy-start.69 = (f32[8,512]{1,0:T(8,128)S(1)}, f32[8,512]{1,0:T(8,128)}, u32[]{:S(2)}) copy-start(f32[8,512]{1,0:T(8,128)} %param.33) | copy-start | bytes 49156
  1576.8 47.7 %copy-start.100 = (f32[8,512]{1,0:T(8,128)S(1)}, f32[8,512]{1,0:T(8,128)}, u32[]{:S(2)}) copy-start(f32[8,512]{1,0:T(8,128)} %param.35) | copy-start | bytes 49156
  1576.8 47.7 %copy-start.101 = (f32[8,512]{1,0:T(8,128)S(1)}, f32[8,512]{1,0:T(8,128)}, u32[]{:S(2)}) copy-start(f32[8,512]{1,0:T(8,128)} %param.34) | copy-start | bytes 49156
  (141 other events, 434.4 us)
Sparse Core Ops, SparseCore 0:
  11.3 153.7 all-gather.2
  1302.9 244.2 reduce-scatter.1
  1551.2 97.3 all-gather.4
where the time goes:
time: 1710 us; the launch traced here: 1700 us
  waiting for transfers between devices  652 us (38%)
  local copies, waits for them, and re-layouts  502 us (29%)
  matrix products  228 us (13%)
  blocking collectives  117 us (7%)
  other arithmetic  104 us (6%)
  loops' own time  47.6 us (3%)
  starting transfers between devices  28.5 us (2%)
  between operations  18.2 us (1%)
    reduce_scatter x1, waiting for transfers between devices, local(): lax.psum_scatter(dense.reshape(-1, tile_width), ('rows', 'seq'), scatter_...  244 us
    all_gather x1, waiting for transfers between devices, local(): lax.all_gather(master_tiles.astype(jnp.bfloat16), 'seq', axis=0, tiled=True)  148 us
    all_to_all x2, waiting for transfers between devices, local(): lax.all_to_all(outgoing, 'seq', split_axis=0, concat_axis=2, tiled=True)  143 us
    dot_general x104, matrix products, right_product(): lax.dot_general(left, right, (((1,), (1,)), ((), ())), preferred_element_...  98.8 us
    all_to_all x1, blocking collectives, local(): lax.all_to_all(packed_grads.reshape(1, group_rows, seq_devices, positions...  74.2 us
    dot_general x72, matrix products, matmul(): return jnp.dot(left, right, preferred_element_type=jnp.float32)  69.5 us
    dot_general x72, matrix products, left_product(): lax.dot_general(left, right, (((0,), (0,)), ((), ())), preferred_element_...  59.3 us
    unnamed x257, local copies, waits for them, and re-layouts  54.6 us
  transfers between devices with their start and end apart: 10, of which 10 were waited for; matrix products, arithmetic and copies ran while one was open for 7% of the time, Pallas kernels for 0%

commit v1 on v0

--- a/solution.py
+++ b/solution.py
@@ -1,6 +1,9 @@
 import jax
 import jax.numpy as jnp
 from jax import lax
+from jax.experimental import pallas as pl
+from jax.experimental.pallas import tpu as pltpu
+
 from jax.sharding import PartitionSpec as P
 
 HEADS = 8
@@ -115,7 +118,7 @@
     return (weight - learn_rate * (update + 0.01 * weight), first, second)
 
 
-def local(
+def local_by_heads(
     residual_in,
     cotangent,
     segments,
@@ -307,36 +310,653 @@
     )
 
 
+F32 = jnp.float32
+BF16 = jnp.bfloat16
+BLOCK = 256
+VMEM_BYTES = 60 * 1024 * 1024
+
+
+def dot_nn(left, right):
+    return jnp.dot(left, right, preferred_element_type=F32)
+
+
+def dot_nt(left, right, precision=None):
+    return lax.dot_general(
+        left, right, (((1,), (1,)), ((), ())), preferred_element_type=F32, precision=precision
+    )
+
+
+def dot_tn(left, right):
+    return lax.dot_general(left, right, (((0,), (0,)), ((), ())), preferred_element_type=F32)
+
+
+def rows_of(number, size=BLOCK):
+    return pl.ds(pl.multiple_of(number * size, size), size)
+
+
+def normalized(values):
+    center = values - jnp.mean(values, axis=-1, keepdims=True)
+    spread = jnp.mean(center * center, axis=-1, keepdims=True)
+    scale = lax.rsqrt(spread + 1e-05)
+    return center * scale, scale
+
+
+GELU_A = 0.7978845608028654
+GELU_B = 0.044715
+
+
+def gelu_value(inner):
+    return 0.5 * inner * (1.0 + jnp.tanh(GELU_A * (inner + GELU_B * inner * inner * inner)))
+
+
+def gelu_both(inner):
+    square = inner * inner
+    bent = jnp.tanh(inner * (GELU_A + GELU_A * GELU_B * square))
+    half = 0.5 + 0.5 * bent
+    slope = half + 0.5 * inner * (1.0 - bent * bent) * (GELU_A + 3.0 * GELU_A * GELU_B * square)
+    return inner * half, slope
+
+
+def weight_copy(tiles, table, number, target, column, row, sem):
+    depth, width = tiles.shape[1], tiles.shape[2]
+    rows = pl.ds(pl.multiple_of(row * depth, depth), depth)
+    columns = pl.ds(pl.multiple_of(column * width, width), width)
+    return pltpu.make_async_copy(
+        tiles.at[table[number]], target.at[rows, columns], sem.at[number]
+    )
+
+
+def weight_group(tiles, table, first, count, per_row, target, sem, act):
+    @pl.loop(0, count)
+    def _(j):
+        copy = weight_copy(
+            tiles, table, first + j, target, lax.rem(j, per_row), lax.div(j, per_row), sem
+        )
+        getattr(copy, act)()
+
+
+def lane_is_first(shape):
+    return lax.broadcasted_iota(jnp.int32, shape, 1) < shape[1] // 2
+
+
+def pair_of(values, lanes_first):
+    zero = jnp.zeros_like(values)
+    return (
+        jnp.where(lanes_first, values, zero).astype(BF16),
+        jnp.where(lanes_first, zero, values).astype(BF16),
+    )
+
+
+def forward_kernel(
+    table, spans, norms, doc_row, doc_col, hidden, tiles,
+    normed_out, packed_out, mixed_out, logsum_out, middle_out, normed_two_out, hidden_out,
+    w_qkv, w_out, w_up, w_down, normed, packed, mixed, logcol, logsum, middle, normed_two, after,
+    w_sem, o_sem,
+):
+    length, width = hidden.shape
+    blocks = length // BLOCK
+    pairs = mixed.shape[0]
+    lanes = mixed.shape[2]
+    groups = (
+        (0, 12, 12, w_qkv), (12, 4, 4, w_out), (16, 16, 16, w_up), (32, 16, 4, w_down),
+    )
+    for first, count, per_row, target in groups:
+        weight_group(tiles, table, first, count, per_row, target, w_sem, "start")
+
+    def ready(group):
+        first, count, per_row, target = groups[group]
+        weight_group(tiles, table, first, count, per_row, target, w_sem, "wait")
+
+    outs = (
+        (normed, normed_out), (packed, packed_out), (mixed, mixed_out), (logsum, logsum_out),
+        (middle, middle_out), (normed_two, normed_two_out), (after, hidden_out),
+    )
+
+    def flush(number):
+        return pltpu.make_async_copy(outs[number][0], outs[number][1], o_sem.at[number])
+
+    ready(0)
+
+    @pl.loop(0, blocks)
+    def _(number):
+        here = rows_of(number)
+        unit, _ = normalized(hidden[here, :])
+        low = (unit * norms[0:1, :] + norms[1:2, :]).astype(BF16)
+        normed[here, :] = low
+        product = dot_nn(low, w_qkv[...])
+        for j in range(3 * pairs):
+            packed[j, here, :] = product[:, j * lanes : (j + 1) * lanes].astype(BF16)
+
+    flush(0).start()
+    flush(1).start()
+    lane_ids = lax.broadcasted_iota(jnp.int32, (BLOCK, lanes), 1)
+    first_half = lane_is_first((BLOCK, lanes))
+
+    @pl.loop(0, blocks)
+    def _(number):
+        here = rows_of(number)
+        low_key = spans[0, number]
+        key_count = spans[1, number]
+        doc_here = doc_col[here, 0:1]
+
+        def with_keys(many):
+            keys_here = pl.ds(pl.multiple_of(low_key * BLOCK, BLOCK), many * BLOCK)
+            same = doc_here == doc_row[0:1, keys_here]
+
+            def one_pair(pair, carry):
+                heads = pair_of(packed[pair, here, :].astype(F32) * 0.125, first_half)
+                keys = packed[pairs + pair, keys_here, :]
+                values = packed[2 * pairs + pair, keys_here, :]
+                results = []
+                logs = logcol[here, :]
+                for side in range(2):
+                    scores = jnp.where(same, dot_nt(heads[side], keys), -1e30)
+                    top = jnp.max(scores, axis=-1, keepdims=True)
+                    weights = jnp.exp(scores - top)
+                    total = jnp.sum(weights, axis=-1, keepdims=True)
+                    results.append(dot_nn(weights.astype(BF16), values) / total)
+                    logs = jnp.where(lane_ids == 8 * pair + side, top + jnp.log(total), logs)
+                mixed[pair, here, :] = jnp.where(first_half, results[0], results[1]).astype(BF16)
+                logcol[here, :] = logs
+                return carry
+
+            lax.fori_loop(0, pairs, one_pair, 0)
+
+        for many in range(1, blocks + 1):
+            pl.when(key_count == many)(lambda many=many: with_keys(many))
+
+    flush(2).start()
+    turned = logcol[...].T
+    for pair in range(pairs):
+        logsum[pair, :, :] = turned[8 * pair : 8 * pair + 8, :]
+    flush(3).start()
+    ready(1)
+    ready(2)
+    ready(3)
+    chunk = width
+
+    @pl.loop(0, blocks)
+    def _(number):
+        here = rows_of(number)
+        side_by_side = jnp.concatenate([mixed[pair, here, :] for pair in range(pairs)], axis=1)
+        mid = hidden[here, :] + dot_nn(side_by_side, w_out[...])
+        middle[here, :] = mid
+        unit, _ = normalized(mid)
+        low = (unit * norms[2:3, :] + norms[3:4, :]).astype(BF16)
+        normed_two[here, :] = low
+        total = mid
+        for c in range(w_up.shape[1] // chunk):
+            part = slice(c * chunk, (c + 1) * chunk)
+            active = gelu_value(dot_nn(low, w_up[:, part])).astype(BF16)
+            total = total + dot_nn(active, w_down[part, :])
+        after[here, :] = total
+
+    flush(4).start()
+    flush(5).start()
+    flush(6).start()
+    for number in range(len(outs)):
+        flush(number).wait()
+
+
+def vmem_spec():
+    return pl.BlockSpec(memory_space=pltpu.VMEM)
+
+
+def any_spec():
+    return pl.BlockSpec(memory_space=pl.ANY)
+
+
+def smem_spec():
+    return pl.BlockSpec(memory_space=pltpu.SMEM)
+
+
+def forward_layer(table, spans, norms, doc_row, doc_col, hidden, tiles, pairs):
+    length, width = hidden.shape
+    lanes = tiles.shape[2]
+    shapes = (
+        ((length, width), BF16),
+        ((3 * pairs, length, lanes), BF16),
+        ((pairs, length, lanes), BF16),
+        ((pairs, 8, length), F32),
+        ((length, width), F32),
+        ((length, width), BF16),
+        ((length, width), F32),
+    )
+    return pl.pallas_call(
+        forward_kernel,
+        name="forward_layer",
+        out_shape=[jax.ShapeDtypeStruct(s, d) for s, d in shapes],
+        in_specs=[smem_spec(), smem_spec()] + [vmem_spec()] * 4 + [any_spec()],
+        out_specs=[any_spec()] * len(shapes),
+        scratch_shapes=[
+            pltpu.VMEM((width, 3 * width), BF16),
+            pltpu.VMEM((width, width), BF16),
+            pltpu.VMEM((width, 4 * width), BF16),
+            pltpu.VMEM((4 * width, width), BF16),
+            pltpu.VMEM(shapes[0][0], BF16),
+            pltpu.VMEM(shapes[1][0], BF16),
+            pltpu.VMEM(shapes[2][0], BF16),
+            pltpu.VMEM((length, lanes), F32),
+            pltpu.VMEM(shapes[3][0], F32),
+            pltpu.VMEM(shapes[4][0], F32),
+            pltpu.VMEM(shapes[5][0], BF16),
+            pltpu.VMEM(shapes[6][0], F32),
+            pltpu.SemaphoreType.DMA((48,)),
+            pltpu.SemaphoreType.DMA((7,)),
+        ],
+        compiler_params=pltpu.CompilerParams(vmem_limit_bytes=VMEM_BYTES),
+        cost_estimate=pl.CostEstimate(
+            flops=length * width * width * 26, bytes_accessed=18 * 2**20,
+            transcendentals=length * length * 4,
+        ),
+    )(table, spans, norms, doc_row, doc_col, hidden, tiles)
+
+
+def backward_kernel(
+    fill, table, spans, counts, norms, doc_row, doc_col, selector,
+    grad_in, normed_in, packed_in, mixed_in, logsum_in, middle_in, normed_two_in, hidden_in, tiles,
+    *rest,
+):
+    rest = list(rest)
+    if not fill:
+        rest.pop(0)
+    (
+        grad_out, tile_grads, norm_grads,
+        w_qkv, w_out, w_up, w_down,
+        grad, normed, packed, mixed, logsum, middle, normed_two, hidden,
+        active, inner_grad, grad_low, mid_grad, mid_low, mixed_grad, delta, packed_grad,
+        key_sum, value_sum, below, staged, blank,
+        w_sem, i_sem, t_sem, z_sem, o_sem,
+    ) = rest
+    length, width = grad.shape
+    blocks = length // BLOCK
+    pairs, lanes = mixed.shape[0], mixed.shape[2]
+    groups = (
+        (0, 12, 12, w_qkv), (12, 4, 4, w_out), (16, 16, 16, w_up), (32, 16, 4, w_down),
+    )
+    ins = (
+        (grad_in, grad), (normed_two_in, normed_two), (middle_in, middle), (mixed_in, mixed),
+        (packed_in, packed), (logsum_in, logsum), (hidden_in, hidden), (normed_in, normed),
+    )
+
+    def load(number):
+        return pltpu.make_async_copy(ins[number][0], ins[number][1], i_sem.at[number])
+
+    def fetch(group, act):
+        first, count, per_row, target = groups[group]
+        weight_group(tiles, table, first, count, per_row, target, w_sem, act)
+
+    load(0).start()
+    load(1).start()
+    fetch(2, "start")
+    fetch(3, "start")
+    load(2).start()
+    fetch(1, "start")
+    load(3).start()
+    load(4).start()
+    load(5).start()
+    fetch(0, "start")
+    load(6).start()
+    load(7).start()
+
+    def blank_copies(act):
+        capacity = tile_grads.shape[0] // counts.shape[0]
+        quarter = capacity // 4
+
+        @pl.loop(0, counts.shape[0])
+        def _(owner):
+            @pl.loop(counts[owner], capacity)
+            def _(place):
+                index = (lax.div(place, quarter) * counts.shape[0] + owner) * quarter + lax.rem(
+                    place, quarter
+                )
+                getattr(
+                    pltpu.make_async_copy(blank, tile_grads.at[index], z_sem.at[index]), act
+                )()
+
+    if fill:
+        blank[...] = jnp.zeros_like(blank)
+        blank_copies("start")
+
+    norm_grads[...] = jnp.zeros_like(norm_grads)
+    load(0).wait()
+    load(1).wait()
+    load(2).wait()
+    fetch(2, "wait")
+    fetch(3, "wait")
+    fetch(1, "wait")
+    load(3).wait()
+    chunk = width
+    chunks = w_up.shape[1] // chunk
+
+    def norm_back(values, out_grad, gain, gain_row):
+        unit, scale = normalized(values)
+        norm_grads[gain_row : gain_row + 1, :] += jnp.sum(out_grad * unit, axis=0, keepdims=True)
+        norm_grads[gain_row + 1 : gain_row + 2, :] += jnp.sum(out_grad, axis=0, keepdims=True)
+        turned = out_grad * gain
+        average = jnp.mean(turned, axis=-1, keepdims=True)
+        along = jnp.mean(turned * unit, axis=-1, keepdims=True)
+        return scale * (turned - average - unit * along)
+
+    @pl.loop(0, blocks)
+    def _(number):
+        here = rows_of(number)
+        upper = grad[here, :]
+        low = upper.astype(BF16)
+        grad_low[here, :] = low
+        normed_here = normed_two[here, :]
+        total = jnp.zeros((BLOCK, width), F32)
+        for c in range(chunks):
+            part = slice(c * chunk, (c + 1) * chunk)
+            value, slope = gelu_both(dot_nn(normed_here, w_up[:, part]))
+            active[here, part] = value.astype(BF16)
+            inner = (slope * dot_nt(low, w_down[part, :])).astype(BF16)
+            inner_grad[here, part] = inner
+            total = total + dot_nt(inner, w_up[:, part])
+        mid = upper + norm_back(middle[here, :], total, norms[2:3, :], 2)
+        mid_grad[here, :] = mid
+        mid_here = mid.astype(BF16)
+        mid_low[here, :] = mid_here
+        back = dot_nt(mid_here, w_out[...]).astype(BF16)
+        for pair in range(pairs):
+            mixed_grad[pair, here, :] = back[:, pair * lanes : (pair + 1) * lanes]
+        side_by_side = jnp.concatenate([mixed[pair, here, :] for pair in range(pairs)], axis=1)
+        both = side_by_side.astype(F32) * back.astype(F32)
+        sums = dot_nt(selector[...], both, precision=lax.Precision.HIGHEST)
+        for pair in range(pairs):
+            delta[pair, :, here] = sums[8 * pair : 8 * pair + 8, :]
+
+    def send_tile(place):
+        return pltpu.make_async_copy(
+            staged.at[place], tile_grads.at[table[place]], t_sem.at[place]
+        )
+
+    def emit(block, first):
+        for c in range(block.shape[1] // lanes):
+            staged[first + c] = block[:, c * lanes : (c + 1) * lanes].astype(BF16)
+            send_tile(first + c).start()
+
+    @pl.loop(0, chunks)
+    def _(c):
+        part = rows_of(c, chunk)
+        emit(dot_tn(active[:, part], grad_low[...]), 32 + 4 * c)
+        emit(dot_tn(normed_two[...], inner_grad[:, part]), 16 + 4 * c)
+
+    side_by_side = jnp.concatenate([mixed[pair] for pair in range(pairs)], axis=1)
+    emit(dot_tn(side_by_side, mid_low[...]), 12)
+    load(4).wait()
+    load(5).wait()
+    first_half = lane_is_first((BLOCK, lanes))
+
+    @pl.loop(0, pairs)
+    def _(pair):
+        key_sum[...] = jnp.zeros_like(key_sum)
+        value_sum[...] = jnp.zeros_like(value_sum)
+
+        @pl.loop(0, blocks)
+        def _(number):
+            here = rows_of(number)
+            low_key = spans[0, number]
+            key_count = spans[1, number]
+            doc_here = doc_row[0:1, here]
+
+            def with_keys(many):
+                keys_here = pl.ds(pl.multiple_of(low_key * BLOCK, BLOCK), many * BLOCK)
+                same = doc_col[keys_here, 0:1] == doc_here
+                heads = pair_of(packed[pair, here, :].astype(F32) * 0.125, first_half)
+                outs = pair_of(mixed_grad[pair, here, :].astype(F32), first_half)
+                keys = packed[pairs + pair, keys_here, :]
+                values = packed[2 * pairs + pair, keys_here, :]
+                query_parts = []
+                key_part = key_sum[keys_here, :]
+                value_part = value_sum[keys_here, :]
+                for side in range(2):
+                    scores = dot_nt(keys, heads[side])
+                    weights = jnp.exp(
+                        jnp.where(same, scores - logsum[pair, side : side + 1, here], -1e30)
+                    )
+                    from_values = dot_nt(values, outs[side])
+                    score_grad = (
+                        weights * (from_values - delta[pair, side : side + 1, here])
+                    ).astype(BF16)
+                    value_part = value_part + dot_nn(weights.astype(BF16), outs[side])
+                    key_part = key_part + dot_nn(score_grad, heads[side])
+                    query_parts.append(dot_tn(score_grad, keys))
+                key_sum[keys_here, :] = key_part
+                value_sum[keys_here, :] = value_part
+                packed_grad[pair, here, :] = (
+                    jnp.where(first_half, query_parts[0], query_parts[1]) * 0.125
+                ).astype(BF16)
+
+            for many in range(1, blocks + 1):
+                pl.when(key_count == many)(lambda many=many: with_keys(many))
+
+        packed_grad[pairs + pair] = key_sum[...].astype(BF16)
+        packed_grad[2 * pairs + pair] = value_sum[...].astype(BF16)
+
+    fetch(0, "wait")
+    load(6).wait()
+    load(7).wait()
+
+    @pl.loop(0, blocks)
+    def _(number):
+        here = rows_of(number)
+        wide = jnp.concatenate([packed_grad[j, here, :] for j in range(3 * pairs)], axis=1)
+        total = dot_nt(wide, w_qkv[...])
+        below[here, :] = mid_grad[here, :] + norm_back(
+            hidden[here, :], total, norms[0:1, :], 0
+        )
+
+    flush = pltpu.make_async_copy(below, grad_out, o_sem.at[0])
+    flush.start()
+
+    @pl.loop(0, 3)
+    def _(c):
+        wide = jnp.concatenate([packed_grad[pairs * c + j] for j in range(pairs)], axis=1)
+        emit(dot_tn(normed[...], wide), 4 * c)
+
+    flush.wait()
+
+    @pl.loop(0, 48)
+    def _(place):
+        send_tile(place).wait()
+
+    if fill:
+        blank_copies("wait")
+
+
+def backward_layer(
+    table, spans, counts, norms, doc_row, doc_col, selector, grad, saved, hidden, tiles, held
+):
+    normed, packed, mixed, logsum, middle, normed_two = saved
+    length, width = grad.shape
+    lanes = tiles.shape[2]
+    pairs = mixed.shape[0]
+    fill = held is None
+
+    def kernel(*refs):
+        backward_kernel(fill, *refs)
+
+    operands = [
+        table, spans, counts, norms, doc_row, doc_col, selector,
+        grad, normed, packed, mixed, logsum, middle, normed_two, hidden, tiles,
+    ]
+    specs = [smem_spec()] * 3 + [vmem_spec()] * 4 + [any_spec()] * 9
+    aliases = {}
+    if not fill:
+        operands.append(held)
+        specs.append(any_spec())
+        aliases = {len(operands) - 1: 1}
+    return pl.pallas_call(
+        kernel,
+        name="backward_layer",
+        out_shape=[
+            jax.ShapeDtypeStruct((length, width), F32),
+            jax.ShapeDtypeStruct(tiles.shape, BF16),
+            jax.ShapeDtypeStruct((4, width), F32),
+        ],
+        in_specs=specs,
+        out_specs=[any_spec(), any_spec(), vmem_spec()],
+        input_output_aliases=aliases,
+        scratch_shapes=[
+            pltpu.VMEM((width, 3 * width), BF16),
+            pltpu.VMEM((width, width), BF16),
+            pltpu.VMEM((width, 4 * width), BF16),
+            pltpu.VMEM((4 * width, width), BF16),
+            pltpu.VMEM((length, width), F32),
+            pltpu.VMEM((length, width), BF16),
+            pltpu.VMEM((3 * pairs, length, lanes), BF16),
+            pltpu.VMEM((pairs, length, lanes), BF16),
+            pltpu.VMEM((pairs, 8, length), F32),
+            pltpu.VMEM((length, width), F32),
+            pltpu.VMEM((length, width), BF16),
+            pltpu.VMEM((length, width), F32),
+            pltpu.VMEM((length, 4 * width), BF16),
+            pltpu.VMEM((length, 4 * width), BF16),
+            pltpu.VMEM((length, width), BF16),
+            pltpu.VMEM((length, width), F32),
+            pltpu.VMEM((length, width), BF16),
+            pltpu.VMEM((pairs, length, lanes), BF16),
+            pltpu.VMEM((pairs, 8, length), F32),
+            pltpu.VMEM((3 * pairs, length, lanes), BF16),
+            pltpu.VMEM((length, lanes), F32),
+            pltpu.VMEM((length, lanes), F32),
+            pltpu.VMEM((length, width), F32),
+            pltpu.VMEM((48, width, lanes), BF16),
+            pltpu.VMEM((width, lanes), BF16),
+            pltpu.SemaphoreType.DMA((48,)),
+            pltpu.SemaphoreType.DMA((8,)),
+            pltpu.SemaphoreType.DMA((48,)),
+            pltpu.SemaphoreType.DMA((tiles.shape[0],)),
+            pltpu.SemaphoreType.DMA((1,)),
+        ],
+        compiler_params=pltpu.CompilerParams(vmem_limit_bytes=VMEM_BYTES),
+        cost_estimate=pl.CostEstimate(
+            flops=length * width * width * 60, bytes_accessed=26 * 2**20,
+            transcendentals=length * length * 4,
+        ),
+    )(*operands)
+
+
+def local_by_rows(
+    residual_in,
+    cotangent,
+    segments,
+    owners,
+    master_tiles,
+    first_tiles,
+    second_tiles,
+    norm_params,
+    norm_first,
+    norm_second,
+):
+    local_rows, positions, model_width = residual_in.shape
+    seq_devices = lax.axis_size("seq")
+    row_devices = lax.axis_size("rows")
+    seq_index = lax.axis_index("seq")
+    row_index = lax.axis_index("rows")
+    length = positions * seq_devices
+    tile_total = owners.shape[0]
+    capacity, _, tile_width = master_tiles.shape
+    quarter = capacity // row_devices
+    pairs = model_width // tile_width
+    places = jnp.arange(tile_total, dtype=jnp.int32)
+    before = (owners[None, :] == owners[:, None]) & (places[None, :] < places[:, None])
+    ranks = jnp.sum(before.astype(jnp.int32), axis=1)
+    table = ((ranks // quarter) * seq_devices + owners) * quarter + ranks % quarter
+    seats = jnp.arange(seq_devices, dtype=jnp.int32)
+    counts = jnp.sum((owners[None, :] == seats[:, None]).astype(jnp.int32), axis=1)
+    mine = lax.dynamic_slice_in_dim(master_tiles, row_index * quarter, quarter, 0)
+    tiles = lax.all_gather(mine.astype(BF16), ("rows", "seq"), axis=0, tiled=True)
+    hidden = lax.all_to_all(residual_in, "seq", split_axis=0, concat_axis=1, tiled=True)[0]
+    upper = lax.all_to_all(cotangent, "seq", split_axis=0, concat_axis=1, tiled=True)[0]
+    doc_ids = lax.dynamic_slice_in_dim(segments, seq_index, 1, 0)
+    doc_row = doc_ids
+    doc_col = jnp.broadcast_to(doc_ids[0][:, None], (length, tile_width))
+    blocks = length // BLOCK
+    firsts = doc_ids[0, ::BLOCK]
+    lasts = doc_ids[0, BLOCK - 1 :: BLOCK]
+    begin = jnp.sum((doc_ids < firsts[:, None]).astype(jnp.int32), axis=1) // BLOCK
+    end = (jnp.sum((doc_ids <= lasts[:, None]).astype(jnp.int32), axis=1) + BLOCK - 1) // BLOCK
+    spans = jnp.stack([begin, end - begin])
+    lane = jnp.arange(model_width)[None, :] // (model_width // HEADS)
+    which = jnp.arange(8 * pairs)[:, None]
+    selector = ((which % 8 < 2) & (lane == 2 * (which // 8) + which % 8)).astype(F32)
+    saved = []
+    for layer_number in range(LAYERS):
+        norms = norm_params[4 * layer_number : 4 * layer_number + 4]
+        part = table[48 * layer_number : 48 * layer_number + 48]
+        *kept, after = forward_layer(part, spans, norms, doc_row, doc_col, hidden, tiles, pairs)
+        saved.append((kept, hidden))
+        hidden = after
+    residual_out = lax.all_to_all(hidden[None], "seq", split_axis=1, concat_axis=0, tiled=True)
+    norm_parts = [None] * LAYERS
+    held = None
+    for layer_number in reversed(range(LAYERS)):
+        norms = norm_params[4 * layer_number : 4 * layer_number + 4]
+        part = table[48 * layer_number : 48 * layer_number + 48]
+        kept, below = saved[layer_number]
+        upper, held, norm_parts[layer_number] = backward_layer(
+            part, spans, counts, norms, doc_row, doc_col, selector, upper, kept, below, tiles, held
+        )
+    input_grad = lax.all_to_all(upper[None], "seq", split_axis=1, concat_axis=0, tiled=True)
+    norm_part = jnp.concatenate(norm_parts, axis=0)
+    piece = lax.psum_scatter(
+        held.reshape(-1, tile_width), ("rows", "seq"), scatter_dimension=0, tiled=True
+    )
+    exact = piece.astype(F32)
+    squares, norm_sum = lax.psum((jnp.sum(exact * exact), norm_part), ("rows", "seq"))
+    owned = lax.all_gather(piece, "rows", axis=0, tiled=True).reshape(master_tiles.shape)
+    keep = (jnp.arange(capacity) < counts[seq_index])[:, None, None]
+    owned = jnp.where(keep, owned.astype(F32), 0.0)
+    total = jnp.sqrt(squares + jnp.sum(norm_sum * norm_sum))
+    factor = 1.0 / jnp.maximum(total, 1.0)
+    clipped = owned * factor
+    norm_clip = norm_sum * factor
+    correction = 1.0 - 0.5**STEP
+    new_weight, new_first_rows, new_second_rows = adamw(
+        master_tiles, clipped, first_tiles, second_tiles, 0.05, correction
+    )
+    new_weight = jnp.where(keep, new_weight, 0.0)
+    new_first_rows = jnp.where(keep, new_first_rows, 0.0)
+    new_second_rows = jnp.where(keep, new_second_rows, 0.0)
+    new_norm, new_norm_f, new_norm_s = adamw(
+        norm_params, norm_clip, norm_first, norm_second, 0.25, correction
+    )
+    return (
+        residual_out,
+        input_grad,
+        clipped,
+        total[None],
+        new_first_rows,
+        new_second_rows,
+        new_weight,
+        new_weight.astype(BF16),
+        norm_clip,
+        new_norm_f,
+        new_norm_s,
+        new_norm,
+    )
+
+
+def local(residual_in, *others):
+    whole_rows = residual_in.shape[0] == lax.axis_size("seq")
+    step = local_by_rows if whole_rows else local_by_heads
+    return step(residual_in, *others)
+
+
 def solution(mesh):
-    placed = (
-        P("rows", "seq", None),
-        P("rows", "seq", None),
-        P("rows", None),
-        P(),
-        P("seq", None, None),
-        P("seq", None, None),
-        P("seq", None, None),
-        P(),
-        P(),
-        P(),
-    )
+    by_rows = P("rows", "seq", None)
+    by_slots = P("seq", None, None)
     return jax.shard_map(
         local,
         mesh=mesh,
-        in_specs=placed,
+        in_specs=(
+            by_rows, by_rows, P("rows", None), P(), by_slots, by_slots, by_slots, P(), P(), P(),
+        ),
         out_specs=(
-            P("rows", "seq", None),
-            P("rows", "seq", None),
-            P("seq", None, None),
-            P(),
-            P("seq", None, None),
-            P("seq", None, None),
-            P("seq", None, None),
-            P("seq", None, None),
-            P(),
-            P(),
-            P(),
-            P(),
+            by_rows, by_rows, by_slots, P(), by_slots, by_slots, by_slots, by_slots,
+            P(), P(), P(), P(),
         ),
         check_vma=False,
     )

time: 1710 us -> 741 us (0.43)
  local copies, waits for them, and re-layouts: 502 us -> 22.4 us
  waiting for transfers between devices: 652 us -> 346 us
  matrix products: 228 us -> 0 us
  Pallas kernels: 0 us -> 185 us
  other arithmetic: 104 us -> 18.7 us
  loops' own time: 47.6 us -> 0 us
    dot_general x248 -> x0, matrix products: 228 us -> none  [the longest x104 98.8 us: right_product(): lax.dot_general(left, right, (((1,), (1,)), ((), ())), preferred_element_...]
    pallas_call x0 -> x4, Pallas kernels: none -> 185 us  [the longest x2 117 us: backward_layer(): pl.pallas_call(kernel, name='backward_layer', out_shape=[jax.ShapeDtypeSt...]
    all_to_all x7 -> x3, waiting for transfers between devices: 237 us -> 75.7 us  [the longest x1 75.7 us: local_by_rows(): lax.all_to_all(hidden[None], 'seq', split_axis=1, concat_axis=0, tiled=True)]
    reshape x27 -> x0, local copies, waits for them, and re-layouts: 130 us -> none  [the longest x4 23.5 us: local(): packed_grads.reshape(1, group_rows, seq_devices, positions * 3 * head_dim)]
    all_gather x2, waiting for transfers between devices: 171 us -> 92.7 us  [the longest x1 92.7 us: local_by_rows(): lax.all_gather(mine.astype(BF16), ('rows', 'seq'), axis=0, tiled=True)]
    transpose x18 -> x0, local copies, waits for them, and re-layouts: 73.7 us -> none  [the longest x2 19.9 us: local(): outgoing.transpose(0, 4, 1, 2, 3, 5)]
    while x100 -> x0, local copies, waits for them, and re-layouts: 67.8 us -> none  [the longest x2 25 us: local(): lax.map(backward_item, (arrived, doc_rows, logsums, head_grads))]
    reduce_scatter x1, waiting for transfers between devices: 244 us -> 178 us  [local_by_rows(): lax.psum_scatter(held.reshape(-1, tile_width), ('rows', 'seq'), scatter_d...]
  transfers between devices with their start and end apart: 10 -> 6, of which waited for: 10 -> 3; matrix products, arithmetic and copies ran while one was open for 7% -> 3% of each run, Pallas kernels for 0% -> 9%
where the time goes in v1:
time: 741 us; the launch traced here: 732 us
  waiting for transfers between devices  346 us (47%)
  Pallas kernels  185 us (25%)
  blocking collectives  131 us (18%)
  local copies, waits for them, and re-layouts  22.4 us (3%)
  other arithmetic  18.7 us (3%)
  between operations  17 us (2%)
  starting transfers between devices  11.7 us (2%)
    reduce_scatter x1, waiting for transfers between devices, local_by_rows(): lax.psum_scatter(held.reshape(-1, tile_width), ('rows', 'seq'), scatter_d...  178 us
    pallas_call x2, Pallas kernels, backward_layer(): pl.pallas_call(kernel, name='backward_layer', out_shape=[jax.ShapeDtypeSt...  117 us
    all_gather x1, waiting for transfers between devices, local_by_rows(): lax.all_gather(mine.astype(BF16), ('rows', 'seq'), axis=0, tiled=True)  92.7 us
    all_to_all x1, blocking collectives, local_by_rows(): lax.all_to_all(residual_in, 'seq', split_axis=0, concat_axis=1, tiled=True)  89 us
    all_to_all x1, waiting for transfers between devices, local_by_rows(): lax.all_to_all(hidden[None], 'seq', split_axis=1, concat_axis=0, tiled=True)  75.7 us
    pallas_call x2, Pallas kernels, forward_layer(): pl.pallas_call(forward_kernel, name='forward_layer', out_shape=[jax.Shape...  68.4 us
    psum x1, blocking collectives, local_by_rows(): lax.psum((jnp.sum(exact * exact), norm_part), ('rows', 'seq'))  42.3 us
  transfers between devices with their start and end apart: 6, of which 3 were waited for; matrix products, arithmetic and copies ran while one was open for 3% of the time, Pallas kernels for 9%

profile of v1, /device:TPU:0, one launch (start us, length us, event | category | flops | bytes accessed | tf_op | source)
XLA Modules:
  0.0 732.1 jit_solution(1089635040555688323)
XLA Ops:
  7.2 2.1 dynamic-slice_convert_fusion
  9.4 89.0 %all_to_all.42 = f32[8,128,512]{2,1,0:T(8,128)} all-to-all(f32[8,128,512]{2,1,0:T(8,128)} %param.10), channel_id=1, replica_groups=mesh['rows'=4,'seq'=8] {'seq'}, dimensions={0} | all-to-all | bytes 4194304 | tf_op jit(solution)/shard_map/all_to_all | solution.py:871
  98.4 3.6 all-to-all-start.2
  105.9 92.7 %all-gather.3.cloned.1.call-done.tiles.refs_15_ = bf16[128,512,128]{2,1,0:T(8,128)(2,1)} async-done(((bf16[4,512,128]{2,1,0:T(8,128)(2,1)}), bf16[128,512,128]{2,1,0:T(8,128)(2,1)}) %all-gather.3.cloned.1.call-update) | async-done | bytes 16777232 | tf_op jit(solution)/shard_map/all_gather | solution.py:870
  198.6 1.0 broadcast_in_dim.47.doc_col.refs_5_
  199.6 34.2 %forward_layer.2 = (bf16[1024,512]{1,0:T(8,128)(2,1)}, bf16[12,1024,128]{2,1,0:T(8,128)(2,1)}, bf16[4,1024,128]{2,1,0:T(8,128)(2,1)}, f32[4,8,1024]{2,1,0:T(8,12...) custom-call(s32[48]{0:T(128)} %get-tuple-element.67.table.refs_0_, ...), custom_call_target="tpu_custom_call" | custom-call | flops 6979321856 | bytes 18874368 | tf_op jit(solution)/shard_map/forward_layer/pallas_call | solution.py:525
  233.8 34.2 %forward_layer.3 = (bf16[1024,512]{1,0:T(8,128)(2,1)}, bf16[12,1024,128]{2,1,0:T(8,128)(2,1)}, bf16[4,1024,128]{2,1,0:T(8,128)(2,1)}, f32[4,8,1024]{2,1,0:T(8,12...) custom-call(s32[48]{0:T(128)} %get-tuple-element.68.table.refs_0_, ...), custom_call_target="tpu_custom_call" | custom-call | flops 6979321856 | bytes 18874368 | tf_op jit(solution)/shard_map/forward_layer/pallas_call | solution.py:525
  268.1 1.3 copy-done.5
  269.4 59.3 %backward_layer.2 = (f32[1024,512]{1,0:T(8,128)}, bf16[128,512,128]{2,1,0:T(8,128)(2,1)}, f32[4,512]{1,0:T(4,128)}) custom-call(s32[48]{0:T(128)} %get-tuple-element.68.table.refs_0_, s32[2,4]{1,0:T(2,128)} %pad_add_fusion.spans.refs_1_, s32[8]{0:T(128)} %convert_reduce_fusion.3.refs_2_, f32[4,512]{1,0:T(4,128)} %get-tuple-element.66.norms.refs_3_, ...), custom_call_target="tpu_custom_call" | custom-call | flops 16106127360 | bytes 27262976 | tf_op jit(solution)/shard_map/backward_layer/pallas_call | solution.py:790
  328.7 57.4 %backward_layer.3 = (f32[1024,512]{1,0:T(8,128)}, bf16[128,512,128]{2,1,0:T(8,128)(2,1)}, f32[4,512]{1,0:T(4,128)}) custom-call(s32[48]{0:T(128)} %get-tuple-element.67.table.refs_0_, s32[2,4]{1,0:T(2,128)} %pad_add_fusion.spans.refs_1_, s32[8]{0:T(128)} %convert_reduce_fusion.3.refs_2_, ...), custom_call_target="tpu_custom_call", output_to_operand_aliasing={{1}: (16, {})} | custom-call | flops 16106127360 | bytes 27262976 | tf_op jit(solution)/shard_map/backward_layer/pallas_call | solution.py:790
  386.1 1.6 copy-done.6
  387.6 3.5 copy.25
  391.1 3.6 all-to-all-start.1
  394.8 5.1 copy.26
  399.8 75.7 %all-to-all-done.1 = f32[1,1024,512]{2,0,1:T(1,128)S(1)} async-done(((f32[1,1024,512]{2,0,1:T(1,128)}), f32[1,1024,512]{2,0,1:T(1,128)S(1)}, u32[]{:S(2)}, u32[]{:S(2)}) %all-to-all-start.1) | async-done | bytes 2097184 | tf_op jit(solution)/shard_map/all_to_all | solution.py:892
  475.5 4.3 all-to-all-start.3
  479.9 177.6 %reduce-scatter.2.cloned.1.call-done = bf16[2048,128]{1,0:T(8,128)(2,1)} async-done(((bf16[65536,128]{1,0:T(8,128)(2,1)}), bf16[2048,128]{1,0:T(8,128)(2,1)}) %reduce-scatter.2.cloned.1.call-update) | async-done | bytes 524304 | tf_op jit(solution)/shard_map/reduce_scatter | solution.py:904
  658.9 1.5 copy.27
  660.4 0.9 multiply_reduce_fusion
  661.2 3.1 copy.28
  664.3 42.3 %all-reduce = (f32[]{:T(128)}, f32[8,512]{1,0:T(8,128)S(1)}) all-reduce(f32[]{:T(128)} %multiply_reduce_fusion, f32[8,512]{1,0:T(8,128)S(1)} %pad_maximum_fusion), channel_id=1, replica_groups=mesh['rows'=4,'seq'=8] {'rows','seq'}, use_global_device_ids=true, to_apply=%region_6.7 | all-reduce | flops 4097 | bytes 32776 | tf_op jit(solution)/shard_map/psum | solution.py:908
  709.2 8.9 %fusion.12 = (bf16[16,512,128]{2,1,0:T(8,128)(2,1)}, f32[16,512,128]{2,1,0:T(8,128)}, f32[16,512,128]{2,1,0:T(8,128)S(1)}) fusion(f32[16,512,128]{2,1,0:T(8,128)} %param.14, f32[16,512,128]{2,1,0:T(8,128)} %param.16, f32[16,512,128]{2,1,0:T(8,128)} %param.15, pred[16]{0:T(512)(128)(4,1)S(1)} %iota_compare_fusion.2, f32[]{:T(128)S(6)} %div.88, ...), kind=kLoop, calls=%fused_computation.60 | loop fusion | flops 19922944 | bytes 25165844 | tf_op jit(solution)/shard_map/convert_element_type | solution.py:934
  718.1 1.2 copy-done.3
  719.3 4.7 broadcast_select_fusion
  (58 shorter events, 6.5 us)
Async XLA Ops:
  7.2 94.9 %copy-start = (s32[8,1024]{1,0:T(8,128)S(1)}, s32[8,1024]{1,0:T(8,128)}, u32[]{:S(2)}) copy-start(s32[8,1024]{1,0:T(8,128)} %param.12) | copy-start | bytes 98308
  7.2 191.4 %all-gather.3.cloned.1.call-start = ((), (), s32[]{:S(2)}) async-start(), calls=%async_computation.5 | async-start | bytes 17301504 | tf_op jit(solution)/shard_map/all_gather | solution.py:870
  9.4 93.8 %copy-start.14 = (s32[96]{0:T(128)S(1)}, s32[96]{0:T(128)}, u32[]{:S(2)}) copy-start(s32[96]{0:T(128)} %param.13) | copy-start | bytes 1156
  9.4 95.2 %copy-start.8 = (f32[8,512]{1,0:T(8,128)S(1)}, f32[8,512]{1,0:T(8,128)}, u32[]{:S(2)}) copy-start(f32[8,512]{1,0:T(8,128)} %param.17) | copy-start | bytes 49156
  98.4 169.7 %all-to-all-start.2 = ((f32[8,128,512]{2,1,0:T(8,128)}), f32[8,128,512]{2,1,0:T(8,128)S(1)}, u32[]{:S(2)}, u32[]{:S(2)}) async-start(f32[8,128,512]{2,1,0:T(8,128)} %param.11), calls=%async_computation.2 | async-start | bytes 4194304 | tf_op jit(solution)/shard_map/all_to_all | solution.py:872
  102.0 555.5 %reduce-scatter.2.cloned.1.call-start = ((), (), s32[]{:S(2)}) async-start(), calls=%async_computation.6 | async-start | bytes 17301504 | tf_op jit(solution)/shard_map/reduce_scatter | solution.py:904
  102.1 97.5 %copy-start.9 = (s32[1,1024]{1,0:T(1,128)}, s32[1,1024]{1,0:T(1,128)S(1)}, u32[]{:S(2)}) copy-start(s32[1,1024]{1,0:T(1,128)S(1)} %constant_dynamic-slice_fusion.doc_row.refs_4_) | copy-start | bytes 12292
  268.1 1.3 copy-start.5
  386.0 1.6 copy-start.6
  391.1 84.4 %all-to-all-start.1 = ((f32[1,1024,512]{2,0,1:T(1,128)}), f32[1,1024,512]{2,0,1:T(1,128)S(1)}, u32[]{:S(2)}, u32[]{:S(2)}) async-start(f32[1,1024,512]{2,0,1:T(1,128)} %copy.25), calls=%async_computation.1 | async-start | bytes 4194304 | tf_op jit(solution)/shard_map/all_to_all | solution.py:892
  394.7 262.8 %copy-start.15 = (s32[8]{0:T(128)S(1)}, s32[8]{0:T(128)}, u32[]{:S(2)}) copy-start(s32[8]{0:T(128)} %convert_reduce_fusion.3.refs_2_) | copy-start | bytes 100
  394.7 264.1 %copy-start.12 = (f32[4,512]{1,0:T(4,128)S(1)}, f32[4,512]{1,0:T(4,128)}, u32[]{:S(2)}) copy-start(f32[4,512]{1,0:T(4,128)} %get-tuple-element.51) | copy-start | bytes 24580
  394.8 264.1 %copy-start.13 = (f32[4,512]{1,0:T(4,128)S(1)}, f32[4,512]{1,0:T(4,128)}, u32[]{:S(2)}) copy-start(f32[4,512]{1,0:T(4,128)} %get-tuple-element.50) | copy-start | bytes 24580
  475.5 185.7 %all-to-all-start.3 = ((f32[1,1024,512]{2,0,1:T(1,128)}), f32[1,1024,512]{2,0,1:T(1,128)}, u32[]{:S(2)}, u32[]{:S(2)}) async-start(f32[1,1024,512]{2,0,1:T(1,128)} %copy.26), calls=%async_computation.3 | async-start | bytes 4194304 | tf_op jit(solution)/shard_map/all_to_all | solution.py:902
  479.9 229.3 %all-gather.5.cloned.1.call-start = ((), (), s32[]{:S(2)}) async-start(), calls=%async_computation.7 | async-start | bytes 2621440 | tf_op jit(solution)/shard_map/all_gather | solution.py:909
  657.5 2.8 copy-start.7
  658.8 49.7 %copy-start.10 = (f32[8,512]{1,0:T(8,128)S(1)}, f32[8,512]{1,0:T(8,128)}, u32[]{:S(2)}) copy-start(f32[8,512]{1,0:T(8,128)} %param.19) | copy-start | bytes 49156
  658.9 49.7 %copy-start.11 = (f32[8,512]{1,0:T(8,128)S(1)}, f32[8,512]{1,0:T(8,128)}, u32[]{:S(2)}) copy-start(f32[8,512]{1,0:T(8,128)} %param.18) | copy-start | bytes 49156
  709.2 8.9 %copy-start.2 = (f32[16,512,128]{2,1,0:T(8,128)S(1)}, f32[16,512,128]{2,1,0:T(8,128)}, u32[]{:S(2)}) copy-start(f32[16,512,128]{2,1,0:T(8,128)} %param.16) | copy-start | bytes 12582916
  709.2 10.1 %copy-start.3 = (f32[16,512,128]{2,1,0:T(8,128)S(1)}, f32[16,512,128]{2,1,0:T(8,128)}, u32[]{:S(2)}) copy-start(f32[16,512,128]{2,1,0:T(8,128)} %param.15) | copy-start | bytes 12582916
  718.1 5.9 copy-start.4
  719.3 4.7 copy-start.1
Sparse Core Ops, SparseCore 0:
  11.6 186.9 all-gather.2
  386.2 271.2 reduce-scatter.1
  659.4 37.4 all-gather.4

commit v2 on v1

--- a/solution.py
+++ b/solution.py
@@ -420,7 +420,7 @@
     @pl.loop(0, blocks)
     def _(number):
         here = rows_of(number)
-        unit, _ = normalized(hidden[here, :])
+        unit, _ = normalized(hidden[here, :].astype(F32))
         low = (unit * norms[0:1, :] + norms[1:2, :]).astype(BF16)
         normed[here, :] = low
         product = dot_nn(low, w_qkv[...])
@@ -479,7 +479,7 @@
     def _(number):
         here = rows_of(number)
         side_by_side = jnp.concatenate([mixed[pair, here, :] for pair in range(pairs)], axis=1)
-        mid = hidden[here, :] + dot_nn(side_by_side, w_out[...])
+        mid = hidden[here, :].astype(F32) + dot_nn(side_by_side, w_out[...])
         middle[here, :] = mid
         unit, _ = normalized(mid)
         low = (unit * norms[2:3, :] + norms[3:4, :]).astype(BF16)
@@ -553,7 +553,7 @@
 
 
 def backward_kernel(
-    fill, table, spans, counts, norms, doc_row, doc_col, selector,
+    fill, table, aims, spans, counts, norms, doc_row, doc_col, selector,
     grad_in, normed_in, packed_in, mixed_in, logsum_in, middle_in, normed_two_in, hidden_in, tiles,
     *rest,
 ):
@@ -607,9 +607,11 @@
         def _(owner):
             @pl.loop(counts[owner], capacity)
             def _(place):
-                index = (lax.div(place, quarter) * counts.shape[0] + owner) * quarter + lax.rem(
-                    place, quarter
-                )
+                core, depth_z, part = lax.rem(owner, 2), lax.div(owner, 2), lax.div(place, quarter)
+                low_bit, high_bit = lax.rem(part, 2), lax.div(part, 2)
+                major = low_bit + core * (high_bit - low_bit)
+                minor = high_bit + core * (low_bit - high_bit)
+                index = lax.rem(place, quarter) * 32 + core * 16 + major * 8 + minor * 4 + depth_z
                 getattr(
                     pltpu.make_async_copy(blank, tile_grads.at[index], z_sem.at[index]), act
                 )()
@@ -641,7 +643,7 @@
     @pl.loop(0, blocks)
     def _(number):
         here = rows_of(number)
-        upper = grad[here, :]
+        upper = grad[here, :].astype(F32)
         low = upper.astype(BF16)
         grad_low[here, :] = low
         normed_here = normed_two[here, :]
@@ -668,7 +670,7 @@
 
     def send_tile(place):
         return pltpu.make_async_copy(
-            staged.at[place], tile_grads.at[table[place]], t_sem.at[place]
+            staged.at[place], tile_grads.at[aims[place]], t_sem.at[place]
         )
 
     def emit(block, first):
@@ -744,7 +746,7 @@
         wide = jnp.concatenate([packed_grad[j, here, :] for j in range(3 * pairs)], axis=1)
         total = dot_nt(wide, w_qkv[...])
         below[here, :] = mid_grad[here, :] + norm_back(
-            hidden[here, :], total, norms[0:1, :], 0
+            hidden[here, :].astype(F32), total, norms[0:1, :], 0
         )
 
     flush = pltpu.make_async_copy(below, grad_out, o_sem.at[0])
@@ -766,7 +768,7 @@
 
 
 def backward_layer(
-    table, spans, counts, norms, doc_row, doc_col, selector, grad, saved, hidden, tiles, held
+    table, aims, spans, counts, norms, doc_row, doc_col, selector, grad, saved, hidden, tiles, held
 ):
     normed, packed, mixed, logsum, middle, normed_two = saved
     length, width = grad.shape
@@ -778,10 +780,10 @@
         backward_kernel(fill, *refs)
 
     operands = [
-        table, spans, counts, norms, doc_row, doc_col, selector,
+        table, aims, spans, counts, norms, doc_row, doc_col, selector,
         grad, normed, packed, mixed, logsum, middle, normed_two, hidden, tiles,
     ]
-    specs = [smem_spec()] * 3 + [vmem_spec()] * 4 + [any_spec()] * 9
+    specs = [smem_spec()] * 4 + [vmem_spec()] * 4 + [any_spec()] * 9
     aliases = {}
     if not fill:
         operands.append(held)
@@ -803,14 +805,14 @@
             pltpu.VMEM((width, width), BF16),
             pltpu.VMEM((width, 4 * width), BF16),
             pltpu.VMEM((4 * width, width), BF16),
-            pltpu.VMEM((length, width), F32),
+            pltpu.VMEM((length, width), grad.dtype),
             pltpu.VMEM((length, width), BF16),
             pltpu.VMEM((3 * pairs, length, lanes), BF16),
             pltpu.VMEM((pairs, length, lanes), BF16),
             pltpu.VMEM((pairs, 8, length), F32),
             pltpu.VMEM((length, width), F32),
             pltpu.VMEM((length, width), BF16),
-            pltpu.VMEM((length, width), F32),
+            pltpu.VMEM((length, width), hidden.dtype),
             pltpu.VMEM((length, 4 * width), BF16),
             pltpu.VMEM((length, 4 * width), BF16),
             pltpu.VMEM((length, width), BF16),
@@ -838,6 +840,400 @@
     )(*operands)
 
 
+MESH_IDS = pl.DeviceIdType.MESH
+
+
+def place_of_device():
+    row = lax.axis_index("rows")
+    seat = lax.axis_index("seq")
+    return row % 2, row // 2, seat // 2, seat % 2
+
+
+def device_at(x, y, z, core):
+    return (2 * y + x, 2 * z + core)
+
+
+def greet(partners):
+    barrier = pltpu.get_barrier_semaphore()
+    for partner in partners:
+        pl.semaphore_signal(barrier, inc=1, device_id=partner, device_id_type=MESH_IDS)
+    pl.semaphore_wait(barrier, len(partners))
+
+
+def seat_partners(x, y, z, core):
+    others = []
+    for k in range(1, 8):
+        seat = (2 * z + core + k) % 8
+        others.append((2 * y + x, seat))
+    return others
+
+
+def post(source, target, send_sem, recv_sem, number, partner):
+    copy = pltpu.make_async_remote_copy(
+        src_ref=source,
+        dst_ref=target,
+        send_sem=send_sem.at[number],
+        recv_sem=recv_sem.at[number],
+        device_id=partner,
+        device_id_type=MESH_IDS,
+    )
+    copy.start()
+    return copy
+
+
+def gather_kernel(master, residual, tiles, rows, wide, low, flat, flat_low, send_sem, recv_sem, l_sem):
+    x, y, z, core = place_of_device()
+    quarter_id = 2 * y + x
+    across = device_at(x, y, z, 1 - core)
+    by_x = device_at(1 - x, y, z, core)
+    by_y = device_at(x, 1 - y, z, core)
+    seats = seat_partners(x, y, z, core)
+    load_near = pltpu.make_async_copy(
+        master.at[pl.ds(4 * quarter_id, 4)], wide.at[pl.ds(4 * quarter_id, 4)], l_sem.at[0]
+    )
+    load_near.start()
+    load_flat = pltpu.make_async_copy(residual, flat, l_sem.at[1])
+    load_flat.start()
+    far = []
+    for k in range(1, 4):
+        part = pl.ds(4 * ((quarter_id + k) % 4), 4)
+        copy = pltpu.make_async_copy(master.at[part], wide.at[part], l_sem.at[1 + k])
+        copy.start()
+        far.append(copy)
+    greet(seats + [by_x, by_y])
+
+    def spot(z_from, quarter):
+        return core * 64 + z_from * 16 + 4 * quarter
+
+    def convert(first, count):
+        @pl.loop(0, count)
+        def _(j):
+            low[first + j] = wide[first + j].astype(BF16)
+
+    sent = []
+    load_near.wait()
+    convert(4 * quarter_id, 4)
+    arrivals = []
+    for k in range(1, 4):
+        z_to = (z + k) % 4
+        here = pl.ds(spot(z, quarter_id), 4)
+        arrivals.append(
+            post(
+                low.at[pl.ds(4 * quarter_id, 4)], tiles.at[here], send_sem, recv_sem, k - 1,
+                device_at(x, y, z_to, core),
+            )
+        )
+    sent += arrivals
+    load_flat.wait()
+
+    @pl.loop(0, flat.shape[0])
+    def _(j):
+        flat_low[j] = flat[j].astype(BF16)
+
+    seat = 2 * z + core
+    row_moves = []
+    for k in range(1, 8):
+        row_moves.append(
+            post(
+                flat_low.at[(seat + k) % 8], rows.at[seat], send_sem, recv_sem, 2 + k,
+                seats[k - 1],
+            )
+        )
+    keep_row = pltpu.make_async_copy(flat_low.at[seat], rows.at[seat], l_sem.at[5])
+    keep_row.start()
+    for k in range(1, 4):
+        far[k - 1].wait()
+        convert(4 * ((quarter_id + k) % 4), 4)
+    mine = pl.ds(core * 64 + z * 16, 16)
+    keep_tiles = pltpu.make_async_copy(low, tiles.at[mine], l_sem.at[6])
+    keep_tiles.start()
+    core_moves = [post(low, tiles.at[mine], send_sem, recv_sem, 10, across)]
+    number = 11
+
+    def relay(part, partner):
+        nonlocal number
+        copy = post(tiles.at[part], tiles.at[part], send_sem, recv_sem, number, partner)
+        number += 1
+        return copy
+
+    x_moves, y_moves, corner_moves = [], [], []
+    quarter_x = 2 * y + (1 - x)
+    quarter_y = 2 * (1 - y) + x
+    for k in range(1, 4):
+        arrivals[k - 1].wait_recv()
+        part = pl.ds(spot((z + 4 - k) % 4, quarter_id), 4)
+        x_moves.append(relay(part, by_x))
+        y_moves.append(relay(part, by_y))
+        core_moves.append(relay(part, across))
+    for k in range(1, 4):
+        z_from = (z + 4 - k) % 4
+        x_moves[k - 1].wait_recv()
+        corner_moves.append(relay(pl.ds(spot(z_from, quarter_x), 2), by_y))
+        core_moves.append(relay(pl.ds(spot(z_from, quarter_x), 4), across))
+        y_moves[k - 1].wait_recv()
+        corner_moves.append(relay(pl.ds(spot(z_from, quarter_y) + 2, 2), by_x))
+        core_moves.append(relay(pl.ds(spot(z_from, quarter_y), 4), across))
+    quarter_c = 3 - quarter_id
+    for k in range(1, 4):
+        z_from = (z + 4 - k) % 4
+        for half in range(2):
+            corner_moves[2 * (k - 1) + half].wait_recv()
+            core_moves.append(relay(pl.ds(spot(z_from, quarter_c) + 2 * half, 2), across))
+    for copy in row_moves + core_moves:
+        copy.wait_recv()
+    for copy in sent + row_moves + core_moves + x_moves + y_moves + corner_moves:
+        copy.wait_send()
+    keep_row.wait()
+    keep_tiles.wait()
+
+
+def gather_start(master_tiles, residual):
+    capacity, depth, lanes = master_tiles.shape
+    count = 3 + 7 + 1 + 9 + 12 + 6
+    return pl.pallas_call(
+        gather_kernel,
+        name="gather_start",
+        out_shape=[
+            jax.ShapeDtypeStruct((8 * capacity, depth, lanes), BF16),
+            jax.ShapeDtypeStruct(residual.shape, BF16),
+        ],
+        in_specs=[any_spec()] * 2,
+        out_specs=[any_spec()] * 2,
+        scratch_shapes=[
+            pltpu.VMEM(master_tiles.shape, F32),
+            pltpu.VMEM(master_tiles.shape, BF16),
+            pltpu.VMEM(residual.shape, F32),
+            pltpu.VMEM(residual.shape, BF16),
+            pltpu.SemaphoreType.DMA((count,)),
+            pltpu.SemaphoreType.DMA((count,)),
+            pltpu.SemaphoreType.DMA((7,)),
+        ],
+        compiler_params=pltpu.CompilerParams(
+            collective_id=0, has_side_effects=True, vmem_limit_bytes=32 * 2**20
+        ),
+        cost_estimate=pl.CostEstimate(
+            flops=0, bytes_accessed=200 * 2**20, transcendentals=0
+        ),
+    )(master_tiles, residual)
+
+
+def reduce_kernel(
+    held, upper, norm_part, owned, rows, norm_sum, squares,
+    core_in, own, one_in, two_in, z_in, piece, flat, flat_low, norm_in, norm_now, square_in,
+    square_now, send_sem, recv_sem, l_sem,
+):
+    x, y, z, core = place_of_device()
+    quarter_id = 2 * y + x
+    across = device_at(x, y, z, 1 - core)
+    by_x = device_at(1 - x, y, z, core)
+    by_y = device_at(x, 1 - y, z, core)
+    by_both = device_at(1 - x, 1 - y, z, core)
+    plus, minus = core, 1 - core
+    first_bit = x * minus + y * plus
+    second_bit = y * minus + x * plus
+    one = device_at(x + minus * (1 - 2 * x), y + plus * (1 - 2 * y), z, core)
+    two = device_at(x + plus * (1 - 2 * x), y + minus * (1 - 2 * y), z, core)
+    along_z = [device_at(x, y, (z + k) % 4, core) for k in range(1, 4)]
+    seats = seat_partners(x, y, z, core)
+    seat = 2 * z + core
+    chunks = own.shape[0]
+    number = 0
+    copies = []
+
+    def move(source, target, partner):
+        nonlocal number
+        copy = post(source, target, send_sem, recv_sem, number, partner)
+        number += 1
+        copies.append(copy)
+        return copy
+
+    loads = []
+    for i in range(chunks):
+        copy = pltpu.make_async_copy(
+            held.at[pl.ds(32 * i + 16 * core, 16)], own.at[i], l_sem.at[i]
+        )
+        copy.start()
+        loads.append(copy)
+    load_flat = pltpu.make_async_copy(upper, flat, l_sem.at[chunks])
+    load_flat.start()
+    greet(seats + [by_x, by_y, by_both])
+    core_moves = [
+        move(held.at[pl.ds(32 * i + 16 * (1 - core), 16)], core_in.at[i], across)
+        for i in range(chunks)
+    ]
+    norm_now[0] = norm_part[...]
+    norm_moves = [move(norm_now.at[0], norm_in.at[0], across)]
+    load_flat.wait()
+
+    @pl.loop(0, flat.shape[0])
+    def _(j):
+        flat_low[j] = flat[j].astype(BF16)
+
+    for k in range(1, 8):
+        move(flat_low.at[(seat + k) % 8], rows.at[seat], seats[k - 1])
+    row_moves = copies[-7:]
+    keep_row = pltpu.make_async_copy(flat_low.at[seat], rows.at[seat], l_sem.at[chunks + 1])
+    keep_row.start()
+
+    def add_in(target, first, incoming, count):
+        @pl.loop(0, count)
+        def _(j):
+            target[first + j] = (
+                target[first + j].astype(F32) + incoming[j].astype(F32)
+            ).astype(BF16)
+
+    one_moves, two_moves, z_moves, plane_moves, keeps = [], [], [], [], []
+
+    def stage_core(i):
+        loads[i].wait()
+        core_moves[i].wait_recv()
+        add_in(own.at[i], 0, core_in.at[i], 16)
+        one_moves.append(
+            move(own.at[i, pl.ds(8 * (1 - first_bit), 8)], one_in.at[i], one)
+        )
+
+    def stage_one(i):
+        one_moves[i].wait_recv()
+        add_in(own.at[i], 8 * first_bit, one_in.at[i], 8)
+        two_moves.append(
+            move(
+                own.at[i, pl.ds(8 * first_bit + 4 * (1 - second_bit), 4)], two_in.at[i], two
+            )
+        )
+
+    def stage_two(i):
+        two_moves[i].wait_recv()
+        base = 8 * first_bit + 4 * second_bit
+        add_in(own.at[i], base, two_in.at[i], 4)
+        z_moves.append(
+            [
+                move(own.at[i, base + (z + k) % 4], z_in.at[i, k - 1], along_z[k - 1])
+                for k in range(1, 4)
+            ]
+        )
+
+    def stage_z(i):
+        for copy in z_moves[i]:
+            copy.wait_recv()
+        total = own[i, 8 * first_bit + 4 * second_bit + z].astype(F32)
+        for k in range(3):
+            total = total + z_in[i, k].astype(F32)
+        piece[i] = total.astype(BF16)
+        square_now[0] += jnp.sum((total * total).reshape(-1, 8, total.shape[1]), axis=0)
+        here = 4 * quarter_id + i
+        for partner in (by_x, by_y, by_both):
+            plane_moves.append(move(piece.at[i], owned.at[here], partner))
+        keep = pltpu.make_async_copy(piece.at[i], owned.at[here], l_sem.at[chunks + 2 + i])
+        keep.start()
+        keeps.append(keep)
+
+    def norm_stage(step, partner):
+        norm_moves[step].wait_recv()
+        norm_now[step + 1] = norm_now[step] + norm_in[step]
+        if partner is not None:
+            norm_moves.append(move(norm_now.at[step + 1], norm_in.at[step + 1], partner))
+
+    square_now[...] = jnp.zeros_like(square_now)
+    stage_core(0)
+    stage_core(1)
+    norm_stage(0, by_x)
+    stage_core(2)
+    stage_core(3)
+    norm_stage(1, by_y)
+    stage_one(0)
+    stage_one(1)
+    norm_stage(2, None)
+    norm_z = [move(norm_now.at[3], norm_in.at[2 + k], along_z[k - 1]) for k in range(1, 4)]
+    stage_two(0)
+    stage_one(2)
+    stage_two(1)
+    stage_z(0)
+    stage_one(3)
+    stage_two(2)
+    stage_z(1)
+    stage_two(3)
+    stage_z(2)
+    stage_z(3)
+
+    def in_order(own_value, incoming):
+        values = [own_value] + [incoming(k) for k in range(1, 4)]
+        total = None
+        for place in range(4):
+            picked = values[0]
+            for k in range(1, 4):
+                picked = jnp.where((z + 4 - k) % 4 == place, values[k], picked)
+            total = picked if total is None else total + picked
+        return total
+
+    square_moves = []
+
+    def square_stage(step, partner):
+        square_moves.append(move(square_now.at[step], square_in.at[step], partner))
+        square_moves[step].wait_recv()
+        square_now[step + 1] = square_now[step] + square_in[step]
+
+    square_stage(0, by_x)
+    square_stage(1, by_y)
+    square_stage(2, across)
+    square_z = [
+        move(square_now.at[3], square_in.at[2 + k], along_z[k - 1]) for k in range(1, 4)
+    ]
+    for copy in norm_z:
+        copy.wait_recv()
+    norm_sum[...] = in_order(norm_now[3], lambda k: norm_in[2 + k])
+    for copy in square_z:
+        copy.wait_recv()
+    squares[...] = in_order(square_now[3], lambda k: square_in[2 + k])
+    for copy in row_moves + plane_moves:
+        copy.wait_recv()
+    for copy in copies:
+        copy.wait_send()
+    keep_row.wait()
+    for keep in keeps:
+        keep.wait()
+
+
+def reduce_end(held, upper, norm_part):
+    slots, depth, lanes = held.shape
+    chunks = 4
+    count = 4 + 1 + 7 + 4 + 4 + 12 + 12 + 2 + 3 + 3 + 3
+    return pl.pallas_call(
+        reduce_kernel,
+        name="reduce_end",
+        out_shape=[
+            jax.ShapeDtypeStruct((slots // 8, depth, lanes), BF16),
+            jax.ShapeDtypeStruct(upper.shape, BF16),
+            jax.ShapeDtypeStruct(norm_part.shape, F32),
+            jax.ShapeDtypeStruct((8, lanes), F32),
+        ],
+        in_specs=[any_spec(), any_spec(), vmem_spec()],
+        out_specs=[any_spec(), any_spec(), vmem_spec(), vmem_spec()],
+        scratch_shapes=[
+            pltpu.VMEM((chunks, 16, depth, lanes), BF16),
+            pltpu.VMEM((chunks, 16, depth, lanes), BF16),
+            pltpu.VMEM((chunks, 8, depth, lanes), BF16),
+            pltpu.VMEM((chunks, 4, depth, lanes), BF16),
+            pltpu.VMEM((chunks, 3, depth, lanes), BF16),
+            pltpu.VMEM((chunks, depth, lanes), BF16),
+            pltpu.VMEM(upper.shape, F32),
+            pltpu.VMEM(upper.shape, BF16),
+            pltpu.VMEM((6, *norm_part.shape), F32),
+            pltpu.VMEM((4, *norm_part.shape), F32),
+            pltpu.VMEM((6, 8, lanes), F32),
+            pltpu.VMEM((4, 8, lanes), F32),
+            pltpu.SemaphoreType.DMA((count,)),
+            pltpu.SemaphoreType.DMA((count,)),
+            pltpu.SemaphoreType.DMA((2 * chunks + 2,)),
+        ],
+        compiler_params=pltpu.CompilerParams(
+            collective_id=1, has_side_effects=True, vmem_limit_bytes=VMEM_BYTES
+        ),
+        cost_estimate=pl.CostEstimate(
+            flops=0, bytes_accessed=300 * 2**20, transcendentals=0
+        ),
+    )(held, upper, norm_part)
+
+
 def local_by_rows(
     residual_in,
     cotangent,
@@ -852,24 +1248,27 @@
 ):
     local_rows, positions, model_width = residual_in.shape
     seq_devices = lax.axis_size("seq")
-    row_devices = lax.axis_size("rows")
     seq_index = lax.axis_index("seq")
-    row_index = lax.axis_index("rows")
     length = positions * seq_devices
     tile_total = owners.shape[0]
     capacity, _, tile_width = master_tiles.shape
-    quarter = capacity // row_devices
+    quarter = capacity // 4
     pairs = model_width // tile_width
     places = jnp.arange(tile_total, dtype=jnp.int32)
     before = (owners[None, :] == owners[:, None]) & (places[None, :] < places[:, None])
     ranks = jnp.sum(before.astype(jnp.int32), axis=1)
-    table = ((ranks // quarter) * seq_devices + owners) * quarter + ranks % quarter
+    core, depth_z, part_id = owners % 2, owners // 2, ranks // quarter
+    major = jnp.where(core == 0, part_id % 2, part_id // 2)
+    minor = jnp.where(core == 0, part_id // 2, part_id % 2)
+    weight_table = core * 64 + depth_z * 16 + ranks
+    grad_table = (ranks % quarter) * 32 + core * 16 + major * 8 + minor * 4 + depth_z
     seats = jnp.arange(seq_devices, dtype=jnp.int32)
     counts = jnp.sum((owners[None, :] == seats[:, None]).astype(jnp.int32), axis=1)
-    mine = lax.dynamic_slice_in_dim(master_tiles, row_index * quarter, quarter, 0)
-    tiles = lax.all_gather(mine.astype(BF16), ("rows", "seq"), axis=0, tiled=True)
-    hidden = lax.all_to_all(residual_in, "seq", split_axis=0, concat_axis=1, tiled=True)[0]
-    upper = lax.all_to_all(cotangent, "seq", split_axis=0, concat_axis=1, tiled=True)[0]
+    tiles, hidden = gather_start(master_tiles, residual_in)
+    hidden = hidden.reshape(length, model_width)
+    later, tiles = lax.optimization_barrier((cotangent, tiles))
+    upper = lax.all_to_all(later.astype(BF16), "seq", split_axis=0, concat_axis=0, tiled=True)
+    upper = upper.reshape(length, model_width)
     doc_ids = lax.dynamic_slice_in_dim(segments, seq_index, 1, 0)
     doc_row = doc_ids
     doc_col = jnp.broadcast_to(doc_ids[0][:, None], (length, tile_width))
@@ -885,31 +1284,31 @@
     saved = []
     for layer_number in range(LAYERS):
         norms = norm_params[4 * layer_number : 4 * layer_number + 4]
-        part = table[48 * layer_number : 48 * layer_number + 48]
+        part = weight_table[48 * layer_number : 48 * layer_number + 48]
         *kept, after = forward_layer(part, spans, norms, doc_row, doc_col, hidden, tiles, pairs)
         saved.append((kept, hidden))
         hidden = after
-    residual_out = lax.all_to_all(hidden[None], "seq", split_axis=1, concat_axis=0, tiled=True)
+    residual_out = lax.all_to_all(
+        hidden.astype(BF16).reshape(residual_in.shape), "seq", split_axis=0, concat_axis=0, tiled=True
+    ).astype(F32)
     norm_parts = [None] * LAYERS
     held = None
     for layer_number in reversed(range(LAYERS)):
         norms = norm_params[4 * layer_number : 4 * layer_number + 4]
-        part = table[48 * layer_number : 48 * layer_number + 48]
+        part = weight_table[48 * layer_number : 48 * layer_number + 48]
+        aims = grad_table[48 * layer_number : 48 * layer_number + 48]
         kept, below = saved[layer_number]
         upper, held, norm_parts[layer_number] = backward_layer(
-            part, spans, counts, norms, doc_row, doc_col, selector, upper, kept, below, tiles, held
-        )
-    input_grad = lax.all_to_all(upper[None], "seq", split_axis=1, concat_axis=0, tiled=True)
+            part, aims, spans, counts, norms, doc_row, doc_col, selector, upper, kept, below, tiles, held
+        )
     norm_part = jnp.concatenate(norm_parts, axis=0)
-    piece = lax.psum_scatter(
-        held.reshape(-1, tile_width), ("rows", "seq"), scatter_dimension=0, tiled=True
-    )
-    exact = piece.astype(F32)
-    squares, norm_sum = lax.psum((jnp.sum(exact * exact), norm_part), ("rows", "seq"))
-    owned = lax.all_gather(piece, "rows", axis=0, tiled=True).reshape(master_tiles.shape)
+    owned, input_grad, norm_sum, squares = reduce_end(
+        held, upper.reshape(residual_in.shape), norm_part
+    )
+    input_grad = input_grad.astype(F32)
     keep = (jnp.arange(capacity) < counts[seq_index])[:, None, None]
     owned = jnp.where(keep, owned.astype(F32), 0.0)
-    total = jnp.sqrt(squares + jnp.sum(norm_sum * norm_sum))
+    total = jnp.sqrt(jnp.sum(squares) + jnp.sum(norm_sum * norm_sum))
     factor = 1.0 / jnp.maximum(total, 1.0)
     clipped = owned * factor
     norm_clip = norm_sum * factor

time: 741 us -> 479 us (0.65)
  waiting for transfers between devices: 346 us -> 0.01 us
  Pallas kernels: 185 us -> 397 us
  blocking collectives: 131 us -> 0 us
  starting transfers between devices: 11.7 us -> 29.9 us
  between operations: 17 us -> 3.8 us
  local copies, waits for them, and re-layouts: 22.4 us -> 9.86 us
  other arithmetic: 18.7 us -> 29.4 us
    pallas_call x0 -> x2, Pallas kernels: none -> 212 us  [the longest x1 126 us: reduce_end(): pl.pallas_call(reduce_kernel, name='reduce_end', out_shape=[jax.ShapeDtyp...]
    reduce_scatter x1 -> x0, waiting for transfers between devices: 178 us -> none  [local_by_rows(): lax.psum_scatter(held.reshape(-1, tile_width), ('rows', 'seq'), scatter_d...]
    all_gather x2 -> x0, waiting for transfers between devices: 92.7 us -> none  [the longest x1 92.7 us: local_by_rows(): lax.all_gather(mine.astype(BF16), ('rows', 'seq'), axis=0, tiled=True)]
    all_to_all x1 -> x0, blocking collectives: 89 us -> none  [local_by_rows(): lax.all_to_all(residual_in, 'seq', split_axis=0, concat_axis=1, tiled=True)]
    all_to_all x3 -> x2, waiting for transfers between devices: 75.7 us -> 0.01 us  [the longest x1 0.01 us: local_by_rows(): lax.all_to_all(later.astype(BF16), 'seq', split_axis=0, concat_axis=0, ti...]
    psum x1 -> x0, blocking collectives: 42.3 us -> none  [local_by_rows(): lax.psum((jnp.sum(exact * exact), norm_part), ('rows', 'seq'))]
    all_to_all x3 -> x2, starting transfers between devices: 11.6 us -> 29.9 us  [the longest x1 25.5 us: local_by_rows(): lax.all_to_all(later.astype(BF16), 'seq', split_axis=0, concat_axis=0, ti...]
    broadcast_in_dim x2 -> x0, local copies, waits for them, and re-layouts: 8.55 us -> none  [the longest x1 5.07 us: local_by_rows(): upper[None]]
  transfers between devices with their start and end apart: 6 -> 2, of which waited for: 3 -> 0; matrix products, arithmetic and copies ran while one was open for 3% -> 6% of each run, Pallas kernels for 9% -> 66%
where the time goes in v2:
time: 479 us; the launch traced here: 470 us
  Pallas kernels  397 us (83%)
  starting transfers between devices  29.9 us (6%)
  other arithmetic  29.4 us (6%)
  local copies, waits for them, and re-layouts  9.86 us (2%)
    pallas_call x1, Pallas kernels, reduce_end(): pl.pallas_call(reduce_kernel, name='reduce_end', out_shape=[jax.ShapeDtyp...  126 us
    pallas_call x2, Pallas kernels, backward_layer(): pl.pallas_call(kernel, name='backward_layer', out_shape=[jax.ShapeDtypeSt...  116 us
    pallas_call x1, Pallas kernels, gather_start(): pl.pallas_call(gather_kernel, name='gather_start', out_shape=[jax.ShapeDt...  85.9 us
    pallas_call x2, Pallas kernels, forward_layer(): pl.pallas_call(forward_kernel, name='forward_layer', out_shape=[jax.Shape...  68 us
    all_to_all x1, starting transfers between devices, local_by_rows(): lax.all_to_all(later.astype(BF16), 'seq', split_axis=0, concat_axis=0, ti...  25.5 us
  transfers between devices with their start and end apart: 2, of which 0 were waited for; matrix products, arithmetic and copies ran while one was open for 6% of the time, Pallas kernels for 66%

profile of v2, /device:TPU:0, one launch (start us, length us, event | category | flops | bytes accessed | tf_op | source)
XLA Modules:
  0.0 469.7 jit_solution(4380367219498141427)
XLA Ops:
  0.7 2.2 copy-done.2
  2.9 1.6 copy-done.3
  4.4 85.9 %gather_start.1 = (bf16[128,512,128]{2,1,0:T(8,128)(2,1)}, bf16[8,128,512]{2,1,0:T(8,128)(2,1)S(1)}) custom-call(f32[16,512,128]{2,1,0:T(8,128)S(1)} %copy-done.2, f32[8,128,512]{2,1,0:T(8,128)S(1)} %copy-done.3), custom_call_target="tpu_custom_call" | custom-call | bytes 209715200 | tf_op jit(solution)/shard_map/gather_start/pallas_call | solution.py:993
  90.4 1.0 copy-done.4
  91.3 1.1 convert_element_type.42
  92.4 25.5 %all-to-all-start.1 = ((bf16[8,128,512]{2,1,0:T(8,128)(2,1)}), bf16[8,128,512]{2,1,0:T(8,128)(2,1)S(1)}, u32[]{:S(2)}, u32[]{:S(2)}) async-start(bf16[8,128,512]{2,1,0:T(8,128)(2,1)} %convert_element_type.42), calls=%async_computation.1 | async-start | bytes 2097152 | tf_op jit(solution)/shard_map/all_to_all | solution.py:1270
  121.2 1.0 broadcast_in_dim.41.doc_col.refs_6_
  122.2 33.8 %forward_layer.2 = (bf16[1024,512]{1,0:T(8,128)(2,1)}, bf16[12,1024,128]{2,1,0:T(8,128)(2,1)}, bf16[4,1024,128]{2,1,0:T(8,128)(2,1)}, f32[4,8,1024]{2,1,0:T(8,12...) custom-call(s32[48]{0:T(128)} %get-tuple-element.91.table.refs_0_, ...), custom_call_target="tpu_custom_call" | custom-call | flops 6979321856 | bytes 18874368 | tf_op jit(solution)/shard_map/forward_layer/pallas_call | solution.py:525
  156.0 34.2 %forward_layer.3 = (bf16[1024,512]{1,0:T(8,128)(2,1)}, bf16[12,1024,128]{2,1,0:T(8,128)(2,1)}, bf16[4,1024,128]{2,1,0:T(8,128)(2,1)}, f32[4,8,1024]{2,1,0:T(8,12...) custom-call(s32[48]{0:T(128)} %get-tuple-element.90.table.refs_0_, ...), custom_call_target="tpu_custom_call" | custom-call | flops 6979321856 | bytes 18874368 | tf_op jit(solution)/shard_map/forward_layer/pallas_call | solution.py:525
  190.2 2.7 convert_element_type.38
  193.6 0.7 and_convert_fusion.refs_7_
  194.4 4.4 all-to-all-start
  198.8 59.0 %backward_layer.2 = (f32[1024,512]{1,0:T(8,128)}, bf16[128,512,128]{2,1,0:T(8,128)(2,1)}, f32[4,512]{1,0:T(4,128)}) custom-call(s32[48]{0:T(128)} %get-tuple-element.90.table.refs_0_, s32[48]{0:T(128)} %get-tuple-element.84.refs_1_, s32[2,4]{1,0:T(2,128)} %pad_add_fusion.spans.refs_2_, s32[8]{0:T(128)} %copy-done.17, ...), custom_call_target="tpu_custom_call" | custom-call | flops 16106127360 | bytes 27262976 | tf_op jit(solution)/shard_map/backward_layer/pallas_call | solution.py:792
  257.8 57.3 %backward_layer.3 = (f32[1024,512]{1,0:T(8,128)}, bf16[128,512,128]{2,1,0:T(8,128)(2,1)}, f32[4,512]{1,0:T(4,128)}) custom-call(s32[48]{0:T(128)} %get-tuple-element.91.table.refs_0_, s32[48]{0:T(128)} %get-tuple-element.85.refs_1_, s32[2,4]{1,0:T(2,128)} %pad_add_fusion.spans.refs_2_, s32[8]{0:T(128)} %copy-done.17, ...), custom_call_target="tpu_custom_call", output_to_operand_aliasing={{1}: (17, {})} | custom-call | flops 16106127360 | bytes 27262976 | tf_op jit(solution)/shard_map/backward_layer/pallas_call | solution.py:792
  315.2 1.3 pad_maximum_fusion.norm_part
  316.5 126.4 %reduce_end.1 = (bf16[16,512,128]{2,1,0:T(8,128)(2,1)}, bf16[8,128,512]{2,1,0:T(8,128)(2,1)}, f32[8,512]{1,0:T(8,128)}, f32[8,128]{1,0:T(8,128)}) custom-call(bf16[128,512,128]{2,1,0:T(8,128)(2,1)} %get-tuple-element.60.held, f32[8,128,512]{2,1,0:T(8,128)} %bitcast.31, f32[8,512]{1,0:T(8,128)} %pad_maximum_fusion.norm_part), custom_call_target="tpu_custom_call" | custom-call | bytes 314572800 | tf_op jit(solution)/shard_map/reduce_end/pallas_call | solution.py:1200
  442.9 1.3 multiply_reduce_fusion
  444.3 1.3 reduce_sum.61
  446.9 3.0 convert_element_type.43
  449.9 1.4 multiply_subtract_fusion
  451.3 8.5 %fusion.17 = (bf16[16,512,128]{2,1,0:T(8,128)(2,1)}, f32[16,512,128]{2,1,0:T(8,128)}, f32[16,512,128]{2,1,0:T(8,128)S(1)}) fusion(f32[16,512,128]{2,1,0:T(8,128)} %master.1, f32[16,512,128]{2,1,0:T(8,128)} %param.16, f32[16,512,128]{2,1,0:T(8,128)} %param.15, pred[16]{0:T(512)(128)(4,1)S(1)} %iota_compare_fusion.2, f32[]{:T(128)S(6)} %div.109, ...), kind=kLoop, calls=%fused_computation.76 | loop fusion | flops 19922944 | bytes 25165844 | tf_op jit(solution)/shard_map/convert_element_type | solution.py:1333
  459.8 2.0 copy-done.7
  461.8 4.7 broadcast_select_fusion
  466.5 1.6 convert_element_type.39
  (51 shorter events, 3.9 us)
Async XLA Ops:
  0.6 117.6 %copy-start = (s32[8,1024]{1,0:T(8,128)S(1)}, s32[8,1024]{1,0:T(8,128)}, u32[]{:S(2)}) copy-start(s32[8,1024]{1,0:T(8,128)} %param.12) | copy-start | bytes 98308
  0.7 2.2 copy-start.2
  2.9 1.6 copy-start.3
  4.4 86.9 %copy-start.9 = (f32[8,128,512]{2,1,0:T(8,128)S(1)}, f32[8,128,512]{2,1,0:T(8,128)}, u32[]{:S(2)}) copy-start(f32[8,128,512]{2,1,0:T(8,128)} %param.11) | copy-start | bytes 6291460
  90.3 1.0 copy-start.4
  91.3 26.7 %copy-start.16 = (s32[96]{0:T(128)S(1)}, s32[96]{0:T(128)}, u32[]{:S(2)}) copy-start(s32[96]{0:T(128)} %param.13) | copy-start | bytes 1156
  91.3 27.8 %copy-start.11 = (f32[8,512]{1,0:T(8,128)S(1)}, f32[8,512]{1,0:T(8,128)}, u32[]{:S(2)}) copy-start(f32[8,512]{1,0:T(8,128)} %param.17) | copy-start | bytes 49156
  92.4 101.9 %all-to-all-start.1 = ((bf16[8,128,512]{2,1,0:T(8,128)(2,1)}), bf16[8,128,512]{2,1,0:T(8,128)(2,1)S(1)}, u32[]{:S(2)}, u32[]{:S(2)}) async-start(bf16[8,128,512]{2,1,0:T(8,128)(2,1)} %convert_element_type.42), calls=%async_computation.1 | async-start | bytes 2097152 | tf_op jit(solution)/shard_map/all_to_all | solution.py:1270
  118.1 37.9 %copy-start.17 = (s32[8]{0:T(128)}, s32[8]{0:T(128)S(1)}, u32[]{:S(2)}) copy-start(s32[8]{0:T(128)S(1)} %convert_reduce_fusion.3.refs_3_) | copy-start | bytes 100
  118.3 3.9 copy-start.12
  194.3 4.4 copy-start.10
  194.4 272.2 %all-to-all-start = ((bf16[8,128,512]{2,1,0:T(8,128)(2,1)}), bf16[8,128,512]{2,1,0:T(8,128)(2,1)S(1)}, u32[]{:S(2)}, u32[]{:S(2)}) async-start(bf16[8,128,512]{2,1,0:T(8,128)(2,1)} %bitcast.6), calls=%async_computation | async-start | bytes 2097152 | tf_op jit(solution)/shard_map/all_to_all | solution.py:1291
  257.8 57.3 %copy-start.15 = (f32[4,512]{1,0:T(4,128)S(1)}, f32[4,512]{1,0:T(4,128)}, u32[]{:S(2)}) copy-start(f32[4,512]{1,0:T(4,128)} %get-tuple-element.63) | copy-start | bytes 24580
  316.5 133.4 %copy-start.13 = (f32[8,512]{1,0:T(8,128)S(1)}, f32[8,512]{1,0:T(8,128)}, u32[]{:S(2)}) copy-start(f32[8,512]{1,0:T(8,128)} %param.19) | copy-start | bytes 49156
  316.5 133.4 %copy-start.14 = (f32[8,512]{1,0:T(8,128)S(1)}, f32[8,512]{1,0:T(8,128)}, u32[]{:S(2)}) copy-start(f32[8,512]{1,0:T(8,128)} %param.18) | copy-start | bytes 49156
  446.9 4.3 copy-start.8
  451.3 10.6 %copy-start.5 = (f32[16,512,128]{2,1,0:T(8,128)S(1)}, f32[16,512,128]{2,1,0:T(8,128)}, u32[]{:S(2)}) copy-start(f32[16,512,128]{2,1,0:T(8,128)} %param.16) | copy-start | bytes 12582916
  451.3 10.6 %copy-start.6 = (f32[16,512,128]{2,1,0:T(8,128)S(1)}, f32[16,512,128]{2,1,0:T(8,128)}, u32[]{:S(2)}) copy-start(f32[16,512,128]{2,1,0:T(8,128)} %param.15) | copy-start | bytes 12582916
  459.8 2.0 copy-start.7
  461.8 6.3 %copy-start.1 = (s32[8,1024]{1,0:T(8,128)S(1)}, s32[8,1024]{1,0:T(8,128)}, u32[]{:S(2)}) copy-start(s32[8,1024]{1,0:T(8,128)} %param.12) | copy-start | bytes 98308

commit v3 on v2

--- a/solution.py
+++ b/solution.py
@@ -313,6 +313,10 @@
 F32 = jnp.float32
 BF16 = jnp.bfloat16
 BLOCK = 256
+DENSE = 1024
+QUERY = 128
+UNROLL = 4
+UNROLL_BACK = 4
 VMEM_BYTES = 60 * 1024 * 1024
 
 
@@ -379,11 +383,14 @@
     return lax.broadcasted_iota(jnp.int32, shape, 1) < shape[1] // 2
 
 
-def pair_of(values, lanes_first):
+def stacked(values, lanes_first):
     zero = jnp.zeros_like(values)
-    return (
-        jnp.where(lanes_first, values, zero).astype(BF16),
-        jnp.where(lanes_first, zero, values).astype(BF16),
+    return jnp.concatenate(
+        [
+            jnp.where(lanes_first, values, zero).astype(BF16),
+            jnp.where(lanes_first, zero, values).astype(BF16),
+        ],
+        axis=0,
     )
 
 
@@ -394,7 +401,7 @@
     w_sem, o_sem,
 ):
     length, width = hidden.shape
-    blocks = length // BLOCK
+    blocks = length // DENSE
     pairs = mixed.shape[0]
     lanes = mixed.shape[2]
     groups = (
@@ -419,7 +426,7 @@
 
     @pl.loop(0, blocks)
     def _(number):
-        here = rows_of(number)
+        here = rows_of(number, DENSE)
         unit, _ = normalized(hidden[here, :].astype(F32))
         low = (unit * norms[0:1, :] + norms[1:2, :]).astype(BF16)
         normed[here, :] = low
@@ -429,40 +436,55 @@
 
     flush(0).start()
     flush(1).start()
-    lane_ids = lax.broadcasted_iota(jnp.int32, (BLOCK, lanes), 1)
-    first_half = lane_is_first((BLOCK, lanes))
-
-    @pl.loop(0, blocks)
+    lane_ids = lax.broadcasted_iota(jnp.int32, (QUERY, lanes), 1)
+    first_half = lane_is_first((QUERY, lanes))
+
+    @pl.loop(0, length // QUERY)
     def _(number):
-        here = rows_of(number)
+        here = rows_of(number, QUERY)
         low_key = spans[0, number]
         key_count = spans[1, number]
         doc_here = doc_col[here, 0:1]
 
         def with_keys(many):
-            keys_here = pl.ds(pl.multiple_of(low_key * BLOCK, BLOCK), many * BLOCK)
+            keys_here = pl.ds(pl.multiple_of(low_key * QUERY, QUERY), many * BLOCK)
             same = doc_here == doc_row[0:1, keys_here]
-
-            def one_pair(pair, carry):
-                heads = pair_of(packed[pair, here, :].astype(F32) * 0.125, first_half)
-                keys = packed[pairs + pair, keys_here, :]
-                values = packed[2 * pairs + pair, keys_here, :]
-                results = []
-                logs = logcol[here, :]
-                for side in range(2):
-                    scores = jnp.where(same, dot_nt(heads[side], keys), -1e30)
-                    top = jnp.max(scores, axis=-1, keepdims=True)
-                    weights = jnp.exp(scores - top)
-                    total = jnp.sum(weights, axis=-1, keepdims=True)
-                    results.append(dot_nn(weights.astype(BF16), values) / total)
-                    logs = jnp.where(lane_ids == 8 * pair + side, top + jnp.log(total), logs)
-                mixed[pair, here, :] = jnp.where(first_half, results[0], results[1]).astype(BF16)
-                logcol[here, :] = logs
-                return carry
-
-            lax.fori_loop(0, pairs, one_pair, 0)
-
-        for many in range(1, blocks + 1):
+            same = jnp.concatenate([same, same], axis=0)
+
+            def score(pair):
+                heads = stacked(packed[pair, here, :].astype(F32) * 0.125, first_half)
+                return dot_nt(heads, packed[pairs + pair, keys_here, :])
+
+            def settle(scores):
+                scores = jnp.where(same, scores, -1e30)
+                top = jnp.max(scores, axis=-1, keepdims=True)
+                weights = jnp.exp(scores - top)
+                total = jnp.sum(weights, axis=-1, keepdims=True)
+                return weights.astype(BF16), total, top + jnp.log(total)
+
+            def finish(pair, weights, total, logs):
+                result = dot_nn(weights, packed[2 * pairs + pair, keys_here, :]) / total
+                mixed[pair, here, :] = jnp.where(
+                    first_half, result[:QUERY], result[QUERY:]
+                ).astype(BF16)
+                old = logcol[here, :]
+                old = jnp.where(lane_ids == 8 * pair, logs[:QUERY], old)
+                logcol[here, :] = jnp.where(lane_ids == 8 * pair + 1, logs[QUERY:], old)
+
+            waiting = None
+            ahead = score(0)
+            for pair in range(pairs):
+                now = ahead
+                if pair + 1 < pairs:
+                    ahead = score(pair + 1)
+                done = settle(now)
+                if waiting is not None:
+                    finish(pair - 1, *waiting)
+                waiting = done
+            finish(pairs - 1, *waiting)
+
+
+        for many in range(1, length // BLOCK + 1):
             pl.when(key_count == many)(lambda many=many: with_keys(many))
 
     flush(2).start()
@@ -477,7 +499,7 @@
 
     @pl.loop(0, blocks)
     def _(number):
-        here = rows_of(number)
+        here = rows_of(number, DENSE)
         side_by_side = jnp.concatenate([mixed[pair, here, :] for pair in range(pairs)], axis=1)
         mid = hidden[here, :].astype(F32) + dot_nn(side_by_side, w_out[...])
         middle[here, :] = mid
@@ -569,7 +591,7 @@
         w_sem, i_sem, t_sem, z_sem, o_sem,
     ) = rest
     length, width = grad.shape
-    blocks = length // BLOCK
+    blocks = length // DENSE
     pairs, lanes = mixed.shape[0], mixed.shape[2]
     groups = (
         (0, 12, 12, w_qkv), (12, 4, 4, w_out), (16, 16, 16, w_up), (32, 16, 4, w_down),
@@ -642,12 +664,12 @@
 
     @pl.loop(0, blocks)
     def _(number):
-        here = rows_of(number)
+        here = rows_of(number, DENSE)
         upper = grad[here, :].astype(F32)
         low = upper.astype(BF16)
         grad_low[here, :] = low
         normed_here = normed_two[here, :]
-        total = jnp.zeros((BLOCK, width), F32)
+        total = jnp.zeros((DENSE, width), F32)
         for c in range(chunks):
             part = slice(c * chunk, (c + 1) * chunk)
             value, slope = gelu_both(dot_nn(normed_here, w_up[:, part]))
@@ -688,53 +710,66 @@
     emit(dot_tn(side_by_side, mid_low[...]), 12)
     load(4).wait()
     load(5).wait()
-    first_half = lane_is_first((BLOCK, lanes))
-
-    @pl.loop(0, pairs)
-    def _(pair):
-        key_sum[...] = jnp.zeros_like(key_sum)
-        value_sum[...] = jnp.zeros_like(value_sum)
-
-        @pl.loop(0, blocks)
-        def _(number):
-            here = rows_of(number)
-            low_key = spans[0, number]
-            key_count = spans[1, number]
-            doc_here = doc_row[0:1, here]
-
-            def with_keys(many):
-                keys_here = pl.ds(pl.multiple_of(low_key * BLOCK, BLOCK), many * BLOCK)
-                same = doc_col[keys_here, 0:1] == doc_here
-                heads = pair_of(packed[pair, here, :].astype(F32) * 0.125, first_half)
-                outs = pair_of(mixed_grad[pair, here, :].astype(F32), first_half)
-                keys = packed[pairs + pair, keys_here, :]
-                values = packed[2 * pairs + pair, keys_here, :]
-                query_parts = []
-                key_part = key_sum[keys_here, :]
-                value_part = value_sum[keys_here, :]
-                for side in range(2):
-                    scores = dot_nt(keys, heads[side])
-                    weights = jnp.exp(
-                        jnp.where(same, scores - logsum[pair, side : side + 1, here], -1e30)
-                    )
-                    from_values = dot_nt(values, outs[side])
-                    score_grad = (
-                        weights * (from_values - delta[pair, side : side + 1, here])
-                    ).astype(BF16)
-                    value_part = value_part + dot_nn(weights.astype(BF16), outs[side])
-                    key_part = key_part + dot_nn(score_grad, heads[side])
-                    query_parts.append(dot_tn(score_grad, keys))
-                key_sum[keys_here, :] = key_part
-                value_sum[keys_here, :] = value_part
-                packed_grad[pair, here, :] = (
-                    jnp.where(first_half, query_parts[0], query_parts[1]) * 0.125
+    first_half = lane_is_first((QUERY, lanes))
+
+    key_sum[...] = jnp.zeros_like(key_sum)
+    value_sum[...] = jnp.zeros_like(value_sum)
+
+    @pl.loop(0, length // QUERY)
+    def _(number):
+        here = rows_of(number, QUERY)
+        low_key = spans[0, number]
+        key_count = spans[1, number]
+        doc_here = doc_row[0:1, here]
+        doc_here = jnp.concatenate([doc_here, doc_here], axis=1)
+
+        def with_keys(many):
+            keys_here = pl.ds(pl.multiple_of(low_key * QUERY, QUERY), many * BLOCK)
+            same = doc_col[keys_here, 0:1] == doc_here
+
+            def score(pair):
+                heads = stacked(packed[pair, here, :].astype(F32) * 0.125, first_half)
+                outs = stacked(mixed_grad[pair, here, :].astype(F32), first_half)
+                return (
+                    heads,
+                    outs,
+                    dot_nt(packed[pairs + pair, keys_here, :], heads),
+                    dot_nt(packed[2 * pairs + pair, keys_here, :], outs),
+                )
+
+            def settle(pair, heads, outs, scores, from_values):
+                logs = jnp.concatenate([logsum[pair, 0:1, here], logsum[pair, 1:2, here]], axis=1)
+                means = jnp.concatenate([delta[pair, 0:1, here], delta[pair, 1:2, here]], axis=1)
+                weights = jnp.exp(jnp.where(same, scores - logs, -1e30))
+                score_grad = (weights * (from_values - means)).astype(BF16)
+                return heads, outs, weights.astype(BF16), score_grad
+
+            def finish(pair, heads, outs, weights, score_grad):
+                value_sum[pair, keys_here, :] += dot_nn(weights, outs)
+                key_sum[pair, keys_here, :] += dot_nn(score_grad, heads)
+                query_part = dot_tn(score_grad, packed[pairs + pair, keys_here, :]) * 0.125
+                packed_grad[pair, here, :] = jnp.where(
+                    first_half, query_part[:QUERY], query_part[QUERY:]
                 ).astype(BF16)
 
-            for many in range(1, blocks + 1):
-                pl.when(key_count == many)(lambda many=many: with_keys(many))
-
-        packed_grad[pairs + pair] = key_sum[...].astype(BF16)
-        packed_grad[2 * pairs + pair] = value_sum[...].astype(BF16)
+            waiting = None
+            ahead = score(0)
+            for pair in range(pairs):
+                now = ahead
+                if pair + 1 < pairs:
+                    ahead = score(pair + 1)
+                done = settle(pair, *now)
+                if waiting is not None:
+                    finish(pair - 1, *waiting)
+                waiting = done
+            finish(pairs - 1, *waiting)
+
+        for many in range(1, length // BLOCK + 1):
+            pl.when(key_count == many)(lambda many=many: with_keys(many))
+
+    for pair in range(pairs):
+        packed_grad[pairs + pair] = key_sum[pair].astype(BF16)
+        packed_grad[2 * pairs + pair] = value_sum[pair].astype(BF16)
 
     fetch(0, "wait")
     load(6).wait()
@@ -742,7 +777,7 @@
 
     @pl.loop(0, blocks)
     def _(number):
-        here = rows_of(number)
+        here = rows_of(number, DENSE)
         wide = jnp.concatenate([packed_grad[j, here, :] for j in range(3 * pairs)], axis=1)
         total = dot_nt(wide, w_qkv[...])
         below[here, :] = mid_grad[here, :] + norm_back(
@@ -821,8 +856,8 @@
             pltpu.VMEM((pairs, length, lanes), BF16),
             pltpu.VMEM((pairs, 8, length), F32),
             pltpu.VMEM((3 * pairs, length, lanes), BF16),
-            pltpu.VMEM((length, lanes), F32),
-            pltpu.VMEM((length, lanes), F32),
+            pltpu.VMEM((pairs, length, lanes), F32),
+            pltpu.VMEM((pairs, length, lanes), F32),
             pltpu.VMEM((length, width), F32),
             pltpu.VMEM((48, width, lanes), BF16),
             pltpu.VMEM((width, lanes), BF16),
@@ -887,19 +922,21 @@
     across = device_at(x, y, z, 1 - core)
     by_x = device_at(1 - x, y, z, core)
     by_y = device_at(x, 1 - y, z, core)
+    quarters = (quarter_id, 2 * y + (1 - x), 2 * (1 - y) + x, 3 - quarter_id)
     seats = seat_partners(x, y, z, core)
+    seat = 2 * z + core
     load_near = pltpu.make_async_copy(
         master.at[pl.ds(4 * quarter_id, 4)], wide.at[pl.ds(4 * quarter_id, 4)], l_sem.at[0]
     )
     load_near.start()
-    load_flat = pltpu.make_async_copy(residual, flat, l_sem.at[1])
-    load_flat.start()
     far = []
     for k in range(1, 4):
         part = pl.ds(4 * ((quarter_id + k) % 4), 4)
         copy = pltpu.make_async_copy(master.at[part], wide.at[part], l_sem.at[1 + k])
         copy.start()
         far.append(copy)
+    load_flat = pltpu.make_async_copy(residual, flat, l_sem.at[1])
+    load_flat.start()
     greet(seats + [by_x, by_y])
 
     def spot(z_from, quarter):
@@ -910,86 +947,138 @@
         def _(j):
             low[first + j] = wide[first + j].astype(BF16)
 
-    sent = []
+    def make(source, target, number, partner):
+        return pltpu.make_async_remote_copy(
+            src_ref=source, dst_ref=target, send_sem=send_sem.at[number],
+            recv_sem=recv_sem.at[number], device_id=partner, device_id_type=MESH_IDS,
+        )
+
+    def relay(number, first, count, partner):
+        part = pl.ds(first, count)
+        return make(tiles.at[part], tiles.at[part], number, partner)
+
+    mine = pl.ds(core * 64 + z * 16, 16)
+    own_here = pl.ds(spot(z, quarter_id), 4)
+
+    def hop(way, step):
+        toward = device_at(x, y, lax.rem(z + (1 if way == 0 else 3), 4), core)
+        number = 3 * way + step - 1
+        if step == 1:
+            return make(low.at[pl.ds(4 * quarter_id, 4)], tiles.at[own_here], number, toward)
+        z_from = lax.rem(z + (5 - step if way == 0 else step - 1), 4)
+        return relay(number, spot(z_from, quarter_id), 4, toward)
+
+    def can_send(way, step):
+        if way == 0:
+            return (z < 3) & (z >= step - 1)
+        return (z > 0) & (z <= 4 - step)
+
+    def arrives(way, step):
+        return z >= step if way == 0 else z <= 3 - step
+
+    def source(way, step):
+        return lax.rem(z + (4 - step if way == 0 else step), 4)
+
+    steps = [(way, step) for step in range(1, 4) for way in range(2)]
+
+    def fan(way, step):
+        base = 6 + 9 * (3 * way + step - 1)
+        z_from = source(way, step)
+        return [
+            relay(base, spot(z_from, quarters[0]), 4, by_x),
+            relay(base + 1, spot(z_from, quarters[0]), 4, by_y),
+            relay(base + 2, spot(z_from, quarters[0]), 4, across),
+            relay(base + 3, spot(z_from, quarters[1]), 2, by_y),
+            relay(base + 4, spot(z_from, quarters[1]), 4, across),
+            relay(base + 5, spot(z_from, quarters[2]) + 2, 2, by_x),
+            relay(base + 6, spot(z_from, quarters[2]), 4, across),
+            relay(base + 7, spot(z_from, quarters[3]), 2, across),
+            relay(base + 8, spot(z_from, quarters[3]) + 2, 2, across),
+        ]
+
     load_near.wait()
     convert(4 * quarter_id, 4)
-    arrivals = []
+    for way in range(2):
+        pl.when(can_send(way, 1))(lambda way=way: hop(way, 1).start())
     for k in range(1, 4):
-        z_to = (z + k) % 4
-        here = pl.ds(spot(z, quarter_id), 4)
-        arrivals.append(
-            post(
-                low.at[pl.ds(4 * quarter_id, 4)], tiles.at[here], send_sem, recv_sem, k - 1,
-                device_at(x, y, z_to, core),
-            )
-        )
-    sent += arrivals
+        far[k - 1].wait()
+        convert(4 * ((quarter_id + k) % 4), 4)
+    keep_tiles = pltpu.make_async_copy(low, tiles.at[mine], l_sem.at[6])
+    keep_tiles.start()
+    own_across = make(low, tiles.at[mine], 60, across)
+    own_across.start()
     load_flat.wait()
 
     @pl.loop(0, flat.shape[0])
     def _(j):
         flat_low[j] = flat[j].astype(BF16)
 
-    seat = 2 * z + core
-    row_moves = []
-    for k in range(1, 8):
-        row_moves.append(
-            post(
-                flat_low.at[(seat + k) % 8], rows.at[seat], send_sem, recv_sem, 2 + k,
-                seats[k - 1],
-            )
-        )
     keep_row = pltpu.make_async_copy(flat_low.at[seat], rows.at[seat], l_sem.at[5])
     keep_row.start()
-    for k in range(1, 4):
-        far[k - 1].wait()
-        convert(4 * ((quarter_id + k) % 4), 4)
-    mine = pl.ds(core * 64 + z * 16, 16)
-    keep_tiles = pltpu.make_async_copy(low, tiles.at[mine], l_sem.at[6])
-    keep_tiles.start()
-    core_moves = [post(low, tiles.at[mine], send_sem, recv_sem, 10, across)]
-    number = 11
-
-    def relay(part, partner):
-        nonlocal number
-        copy = post(tiles.at[part], tiles.at[part], send_sem, recv_sem, number, partner)
-        number += 1
-        return copy
-
-    x_moves, y_moves, corner_moves = [], [], []
-    quarter_x = 2 * y + (1 - x)
-    quarter_y = 2 * (1 - y) + x
-    for k in range(1, 4):
-        arrivals[k - 1].wait_recv()
-        part = pl.ds(spot((z + 4 - k) % 4, quarter_id), 4)
-        x_moves.append(relay(part, by_x))
-        y_moves.append(relay(part, by_y))
-        core_moves.append(relay(part, across))
-    for k in range(1, 4):
-        z_from = (z + 4 - k) % 4
-        x_moves[k - 1].wait_recv()
-        corner_moves.append(relay(pl.ds(spot(z_from, quarter_x), 2), by_y))
-        core_moves.append(relay(pl.ds(spot(z_from, quarter_x), 4), across))
-        y_moves[k - 1].wait_recv()
-        corner_moves.append(relay(pl.ds(spot(z_from, quarter_y) + 2, 2), by_x))
-        core_moves.append(relay(pl.ds(spot(z_from, quarter_y), 4), across))
-    quarter_c = 3 - quarter_id
-    for k in range(1, 4):
-        z_from = (z + 4 - k) % 4
-        for half in range(2):
-            corner_moves[2 * (k - 1) + half].wait_recv()
-            core_moves.append(relay(pl.ds(spot(z_from, quarter_c) + 2 * half, 2), across))
-    for copy in row_moves + core_moves:
+    row_moves = [
+        make(flat_low.at[(seat + k) % 8], rows.at[seat], 60 + k, seats[k - 1])
+        for k in range(1, 8)
+    ]
+
+    def take(way, step):
+        hop(way, step).wait_recv()
+        if step < 3:
+            pl.when(can_send(way, step + 1))(lambda: hop(way, step + 1).start())
+        for copy in fan(way, step)[:3]:
+            copy.start()
+
+    def turn(way, step):
+        moves = fan(way, step)
+        moves[0].wait_recv()
+        moves[3].start()
+        moves[4].start()
+        moves[1].wait_recv()
+        moves[5].start()
+        moves[6].start()
+
+    def finish(way, step):
+        moves = fan(way, step)
+        moves[3].wait_recv()
+        moves[7].start()
+        moves[5].wait_recv()
+        moves[8].start()
+
+    def drain(way, step):
+        moves = fan(way, step)
+        for number in (2, 4, 6, 7, 8):
+            moves[number].wait_recv()
+        for copy in moves:
+            copy.wait_send()
+
+    def each(act, chosen):
+        for way, step in chosen:
+            pl.when(arrives(way, step))(lambda way=way, step=step: act(way, step))
+
+    each(take, steps[:2])
+    each(take, steps[2:4])
+    each(turn, steps[:2])
+    each(take, steps[4:])
+    for copy in row_moves:
+        copy.start()
+    each(turn, steps[2:4])
+    each(finish, steps[:2])
+    each(turn, steps[4:])
+    each(finish, steps[2:])
+    own_across.wait_recv()
+    each(drain, steps)
+    for way, step in steps:
+        pl.when(can_send(way, step))(lambda way=way, step=step: hop(way, step).wait_send())
+    for copy in row_moves:
         copy.wait_recv()
-    for copy in sent + row_moves + core_moves + x_moves + y_moves + corner_moves:
         copy.wait_send()
+    own_across.wait_send()
     keep_row.wait()
     keep_tiles.wait()
 
 
 def gather_start(master_tiles, residual):
     capacity, depth, lanes = master_tiles.shape
-    count = 3 + 7 + 1 + 9 + 12 + 6
+    count = 68
     return pl.pallas_call(
         gather_kernel,
         name="gather_start",
@@ -1009,7 +1098,7 @@
             pltpu.SemaphoreType.DMA((7,)),
         ],
         compiler_params=pltpu.CompilerParams(
-            collective_id=0, has_side_effects=True, vmem_limit_bytes=32 * 2**20
+            collective_id=0, has_side_effects=True, vmem_limit_bytes=VMEM_BYTES
         ),
         cost_estimate=pl.CostEstimate(
             flops=0, bytes_accessed=200 * 2**20, transcendentals=0
@@ -1272,12 +1361,10 @@
     doc_ids = lax.dynamic_slice_in_dim(segments, seq_index, 1, 0)
     doc_row = doc_ids
     doc_col = jnp.broadcast_to(doc_ids[0][:, None], (length, tile_width))
-    blocks = length // BLOCK
-    firsts = doc_ids[0, ::BLOCK]
-    lasts = doc_ids[0, BLOCK - 1 :: BLOCK]
-    begin = jnp.sum((doc_ids < firsts[:, None]).astype(jnp.int32), axis=1) // BLOCK
-    end = (jnp.sum((doc_ids <= lasts[:, None]).astype(jnp.int32), axis=1) + BLOCK - 1) // BLOCK
-    spans = jnp.stack([begin, end - begin])
+    begin = jnp.sum((doc_ids < doc_ids[0, ::QUERY, None]).astype(jnp.int32), axis=1) // QUERY
+    end = jnp.sum((doc_ids <= doc_ids[0, QUERY - 1 :: QUERY, None]).astype(jnp.int32), axis=1)
+    many = (end - begin * QUERY + BLOCK - 1) // BLOCK
+    spans = jnp.stack([jnp.minimum(begin, (length - many * BLOCK) // QUERY), many])
     lane = jnp.arange(model_width)[None, :] // (model_width // HEADS)
     which = jnp.arange(8 * pairs)[:, None]
     selector = ((which % 8 < 2) & (lane == 2 * (which // 8) + which % 8)).astype(F32)

time: 479 us -> 404 us (0.84)
  the two profiles are of different devices: /device:TPU:0 before, /device:TPU:2 now
where the time goes in v3:
time: 404 us; the launch traced here: 397 us
  Pallas kernels  351 us (87%)
  other arithmetic  29.4 us (7%)
  starting transfers between devices  7.61 us (2%)
  local copies, waits for them, and re-layouts  5.09 us (1%)
    pallas_call x1, Pallas kernels, reduce_end(): pl.pallas_call(reduce_kernel, name='reduce_end', out_shape=[jax.ShapeDtyp...  126 us
    pallas_call x2, Pallas kernels, backward_layer(): pl.pallas_call(kernel, name='backward_layer', out_shape=[jax.ShapeDtypeSt...  102 us
    pallas_call x1, Pallas kernels, gather_start(): pl.pallas_call(gather_kernel, name='gather_start', out_shape=[jax.ShapeDt...  74.5 us
    pallas_call x2, Pallas kernels, forward_layer(): pl.pallas_call(forward_kernel, name='forward_layer', out_shape=[jax.Shape...  49 us
    convert_element_type x1, other arithmetic, local_by_rows(): new_weight.astype(BF16)  8.54 us
  transfers between devices with their start and end apart: 2, of which 0 were waited for; matrix products, arithmetic and copies ran while one was open for 7% of the time, Pallas kernels for 70%

profile of v3, /device:TPU:2, one launch (start us, length us, event | category | flops | bytes accessed | tf_op | source)
XLA Modules:
  0.0 397.0 jit_solution(4906542944337617613)
XLA Ops:
  0.7 74.5 %gather_start.1 = (bf16[128,512,128]{2,1,0:T(8,128)(2,1)}, bf16[8,128,512]{2,1,0:T(8,128)(2,1)}) custom-call(f32[16,512,128]{2,1,0:T(8,128)} %master.1, f32[8,128,512]{2,1,0:T(8,128)} %residual.1), custom_call_target="tpu_custom_call" | custom-call | bytes 209715200 | tf_op jit(solution)/shard_map/gather_start/pallas_call | solution.py:1082
  75.2 1.1 convert_element_type.42
  76.3 3.6 all-to-all-start.1
  81.0 0.6 fusion.19
  81.6 0.6 fusion.20
  83.1 1.0 broadcast_in_dim.41.doc_col.refs_6_
  84.1 24.2 %forward_layer.2 = (bf16[1024,512]{1,0:T(8,128)(2,1)}, bf16[12,1024,128]{2,1,0:T(8,128)(2,1)}, bf16[4,1024,128]{2,1,0:T(8,128)(2,1)}, f32[4,8,1024]{2,1,0:T(8,12...) custom-call(s32[48]{0:T(128)} %get-tuple-element.91.table.refs_0_, ...), custom_call_target="tpu_custom_call" | custom-call | flops 6979321856 | bytes 18874368 | tf_op jit(solution)/shard_map/forward_layer/pallas_call | solution.py:547
  108.4 24.8 %forward_layer.3 = (bf16[1024,512]{1,0:T(8,128)(2,1)}, bf16[12,1024,128]{2,1,0:T(8,128)(2,1)}, bf16[4,1024,128]{2,1,0:T(8,128)(2,1)}, f32[4,8,1024]{2,1,0:T(8,12...) custom-call(s32[48]{0:T(128)} %get-tuple-element.90.table.refs_0_, ...), custom_call_target="tpu_custom_call" | custom-call | flops 6979321856 | bytes 18874368 | tf_op jit(solution)/shard_map/forward_layer/pallas_call | solution.py:547
  133.1 2.7 convert_element_type.38
  135.9 0.7 iota_compare_fusion.2
  136.5 0.7 and_convert_fusion.refs_7_
  137.2 4.1 %all-to-all-start = ((bf16[8,128,512]{2,1,0:T(8,128)(2,1)}), bf16[8,128,512]{2,1,0:T(8,128)(2,1)S(1)}, u32[]{:S(2)}, u32[]{:S(2)}) async-start(bf16[8,128,512]{2,1,0:T(8,128)(2,1)} %bitcast.6), calls=%async_computation | async-start | bytes 2097152 | tf_op jit(solution)/shard_map/all_to_all | solution.py:1378
  141.3 52.1 %backward_layer.2 = (f32[1024,512]{1,0:T(8,128)}, bf16[128,512,128]{2,1,0:T(8,128)(2,1)}, f32[4,512]{1,0:T(4,128)}) custom-call(s32[48]{0:T(128)} %get-tuple-element.90.table.refs_0_, s32[48]{0:T(128)} %get-tuple-element.86.refs_1_, s32[2,8]{1,0:T(2,128)} %pad_add_fusion.spans.refs_2_, s32[8]{0:T(128)} %copy-done.14, ...), custom_call_target="tpu_custom_call" | custom-call | flops 16106127360 | bytes 27262976 | tf_op jit(solution)/shard_map/backward_layer/pallas_call | solution.py:827
  193.5 50.1 %backward_layer.3 = (f32[1024,512]{1,0:T(8,128)}, bf16[128,512,128]{2,1,0:T(8,128)(2,1)}, f32[4,512]{1,0:T(4,128)}) custom-call(s32[48]{0:T(128)} %get-tuple-element.91.table.refs_0_, s32[48]{0:T(128)} %get-tuple-element.87.refs_1_, s32[2,8]{1,0:T(2,128)} %pad_add_fusion.spans.refs_2_, s32[8]{0:T(128)} %copy-done.14, ...), custom_call_target="tpu_custom_call", output_to_operand_aliasing={{1}: (17, {})} | custom-call | flops 16106127360 | bytes 27262976 | tf_op jit(solution)/shard_map/backward_layer/pallas_call | solution.py:827
  243.5 1.3 pad_maximum_fusion.norm_part
  244.9 125.6 %reduce_end.1 = (bf16[16,512,128]{2,1,0:T(8,128)(2,1)}, bf16[8,128,512]{2,1,0:T(8,128)(2,1)}, f32[8,512]{1,0:T(8,128)}, f32[8,128]{1,0:T(8,128)}) custom-call(bf16[128,512,128]{2,1,0:T(8,128)(2,1)} %get-tuple-element.60.held, f32[8,128,512]{2,1,0:T(8,128)} %bitcast.31, f32[8,512]{1,0:T(8,128)} %pad_maximum_fusion.norm_part), custom_call_target="tpu_custom_call" | custom-call | bytes 314572800 | tf_op jit(solution)/shard_map/reduce_end/pallas_call | solution.py:1289
  370.5 1.3 multiply_reduce_fusion
  371.8 1.3 reduce_sum.64
  374.5 3.0 convert_element_type.43
  377.5 1.4 multiply_subtract_fusion
  378.8 8.5 %fusion.18 = (bf16[16,512,128]{2,1,0:T(8,128)(2,1)}, f32[16,512,128]{2,1,0:T(8,128)}, f32[16,512,128]{2,1,0:T(8,128)S(1)}) fusion(f32[16,512,128]{2,1,0:T(8,128)} %master.1, f32[16,512,128]{2,1,0:T(8,128)} %param.16, f32[16,512,128]{2,1,0:T(8,128)} %param.15, pred[16]{0:T(512)(128)(4,1)S(1)} %iota_compare_fusion.2, f32[]{:T(128)S(6)} %div.123, ...), kind=kLoop, calls=%fused_computation.81 | loop fusion | flops 19922944 | bytes 25165844 | tf_op jit(solution)/shard_map/convert_element_type | solution.py:1420
  387.4 2.0 copy-done.4
  389.4 4.7 %broadcast_select_fusion = (f32[16,512,128]{2,1,0:T(8,128)}, f32[16,512,128]{2,1,0:T(8,128)}) fusion(pred[16]{0:T(512)(128)(4,1)S(1)} %iota_compare_fusion.2, f32[16,512,128]{2,1,0:T(8,128)S(1)} %get-tuple-element.76, f32[16,512,128]{2,1,0:T(8,128)S(1)} %copy-done.2, f32[16,512,128]{2,1,0:T(8,128)S(1)} %copy-done.3), kind=kLoop, calls=%fused_computation.5 | loop fusion | flops 8388608 | bytes 20971536 | tf_op jit(solution)/shard_map/jit(_where)/select_n | solution.py:1408
  394.1 1.6 convert_element_type.39
  (45 shorter events, 2.0 us)
Async XLA Ops:
  0.6 79.5 %copy-start = (s32[8,1024]{1,0:T(8,128)S(1)}, s32[8,1024]{1,0:T(8,128)}, u32[]{:S(2)}) copy-start(s32[8,1024]{1,0:T(8,128)} %param.12) | copy-start | bytes 98308
  0.7 74.5 %copy-start.6 = (f32[8,128,512]{2,1,0:T(8,128)S(1)}, f32[8,128,512]{2,1,0:T(8,128)}, u32[]{:S(2)}) copy-start(f32[8,128,512]{2,1,0:T(8,128)} %param.11) | copy-start | bytes 6291460
  75.1 4.7 %copy-start.13 = (s32[96]{0:T(128)S(1)}, s32[96]{0:T(128)}, u32[]{:S(2)}) copy-start(s32[96]{0:T(128)} %param.13) | copy-start | bytes 1156
  75.1 5.9 %copy-start.8 = (f32[8,512]{1,0:T(8,128)S(1)}, f32[8,512]{1,0:T(8,128)}, u32[]{:S(2)}) copy-start(f32[8,512]{1,0:T(8,128)} %param.17) | copy-start | bytes 49156
  76.3 61.0 %all-to-all-start.1 = ((bf16[8,128,512]{2,1,0:T(8,128)(2,1)}), bf16[8,128,512]{2,1,0:T(8,128)(2,1)S(1)}, u32[]{:S(2)}, u32[]{:S(2)}) async-start(bf16[8,128,512]{2,1,0:T(8,128)(2,1)} %convert_element_type.42), calls=%async_computation.1 | async-start | bytes 2097152 | tf_op jit(solution)/shard_map/all_to_all | solution.py:1359
  80.0 28.4 %copy-start.14 = (s32[8]{0:T(128)}, s32[8]{0:T(128)S(1)}, u32[]{:S(2)}) copy-start(s32[8]{0:T(128)S(1)} %convert_reduce_fusion.3.refs_3_) | copy-start | bytes 100
  80.2 3.9 copy-start.9
  137.2 4.1 %copy-start.7 = (bf16[8,128,512]{2,1,0:T(8,128)(2,1)}, bf16[8,128,512]{2,1,0:T(8,128)(2,1)S(1)}, u32[]{:S(2)}) copy-start(bf16[8,128,512]{2,1,0:T(8,128)(2,1)S(1)} %all-to-all-done.1) | copy-start | bytes 3145732
  137.2 256.8 %all-to-all-start = ((bf16[8,128,512]{2,1,0:T(8,128)(2,1)}), bf16[8,128,512]{2,1,0:T(8,128)(2,1)S(1)}, u32[]{:S(2)}, u32[]{:S(2)}) async-start(bf16[8,128,512]{2,1,0:T(8,128)(2,1)} %bitcast.6), calls=%async_computation | async-start | bytes 2097152 | tf_op jit(solution)/shard_map/all_to_all | solution.py:1378
  193.5 50.1 %copy-start.12 = (f32[4,512]{1,0:T(4,128)S(1)}, f32[4,512]{1,0:T(4,128)}, u32[]{:S(2)}) copy-start(f32[4,512]{1,0:T(4,128)} %get-tuple-element.63) | copy-start | bytes 24580
  244.9 132.6 %copy-start.10 = (f32[8,512]{1,0:T(8,128)S(1)}, f32[8,512]{1,0:T(8,128)}, u32[]{:S(2)}) copy-start(f32[8,512]{1,0:T(8,128)} %param.19) | copy-start | bytes 49156
  244.9 132.6 %copy-start.11 = (f32[8,512]{1,0:T(8,128)S(1)}, f32[8,512]{1,0:T(8,128)}, u32[]{:S(2)}) copy-start(f32[8,512]{1,0:T(8,128)} %param.18) | copy-start | bytes 49156
  374.5 4.3 %copy-start.5 = (bf16[16,512,128]{2,1,0:T(8,128)(2,1)S(1)}, bf16[16,512,128]{2,1,0:T(8,128)(2,1)}, u32[]{:S(2)}) copy-start(bf16[16,512,128]{2,1,0:T(8,128)(2,1)} %get-tuple-element.65) | copy-start | bytes 6291460
  378.8 10.6 %copy-start.2 = (f32[16,512,128]{2,1,0:T(8,128)S(1)}, f32[16,512,128]{2,1,0:T(8,128)}, u32[]{:S(2)}) copy-start(f32[16,512,128]{2,1,0:T(8,128)} %param.16) | copy-start | bytes 12582916
  378.8 10.6 %copy-start.3 = (f32[16,512,128]{2,1,0:T(8,128)S(1)}, f32[16,512,128]{2,1,0:T(8,128)}, u32[]{:S(2)}) copy-start(f32[16,512,128]{2,1,0:T(8,128)} %param.15) | copy-start | bytes 12582916
  387.4 2.0 copy-start.4
  389.4 6.3 %copy-start.1 = (s32[8,1024]{1,0:T(8,128)S(1)}, s32[8,1024]{1,0:T(8,128)}, u32[]{:S(2)}) copy-start(s32[8,1024]{1,0:T(8,128)} %param.12) | copy-start | bytes 98308
